TPU v7x, 128 devices: a whole 4x4x4 slice. The times are simulated.
128 devices in a mesh: row: 4 (over y), col: 32 (over z, x, core).
Axes of the slice: x: 4, y: 4, z: 4, core: 2. Of those that a mesh axis runs over, the one named last changes fastest.
Arguments:
- src_cent: float32 [16, 4096], P(None, 'row'), may hold values from -6.5 to 6.5
- tgt_cent: float32 [16, 4096], P(None, 'col'), may hold values from -6.5 to 6.5
- src_mass: float32 [4096], P('row'), may hold values from 6.1035156e-05 to 0.0009765625
- tgt_mass: float32 [4096], P('col'), may hold values from 6.1035156e-05 to 0.0009765625
- src_pts: float32 [16, 262144], P(None, ('row', 'col')), may hold values from -6.5 to 6.5
- tgt_pts: float32 [16, 1048576], P(None, ('row', 'col')), may hold values from -6.5 to 6.5
- src_cluster: int32 [262144], P(('row', 'col')), may hold values from 0 to 4095
- tgt_cluster: int32 [1048576], P(('row', 'col')), may hold values from 0 to 4095
- support: int32 [1024, 16], P(('row', 'col')), may hold values from 0 to 4095, as said below
Outputs:
- coarse_f: float32 [4096], P('row')
- coarse_g: float32 [4096], P('col')
- fine_f: float32 [262144], P(('row', 'col'))
- fine_g: float32 [1048576], P(('row', 'col'))
Inputs may be any that keep to these rules, and one draw needn't show every extreme that they name: `support`: each row names 16 different target blocks; every target block is named by some row; among the rows of one device (aligned blocks of 8 rows) at most 2 entries fall in any one range k * 32 to (k + 1) * 32 - 1, and exactly 2 in some such range for every device.
All inputs are finite; a program needn't handle non-finite values.
Results may differ from a plain program's by a relative error of at most 0.0003.
Values sent between devices are 32-bit elements; how exact they have to be, the bound alone decides.
A program may use at most 64 MiB of HBM per device.

v0:
```python
import jax
import jax.numpy as jnp
from jax import lax
from jax.sharding import PartitionSpec as P

F = 16
BLK = 256
SUPP = 16
ITERS = 8
SB_DEV = 8
TB_DEV = 32


EPS = 0.1


def combined_all(x, axis, combine):
    everything = jax.tree.map(lambda part: lax.all_gather(part, axis), x)
    leading = jax.tree.map(lambda part: part[0], everything)

    def hop(k, so_far):
        return combine(so_far, jax.tree.map(lambda part: part[k], everything))

    return lax.fori_loop(1, lax.axis_size(axis), hop, leading)


def pair_cost(left_pts, right_pts):
    cross = jnp.einsum(
        "fi,fj->ij",
        left_pts,
        right_pts,
        precision=lax.Precision.HIGHEST,
        preferred_element_type=jnp.float32,
    )
    return (
        jnp.sum(left_pts * left_pts, 0)[:, None]
        + jnp.sum(right_pts * right_pts, 0)[None, :]
        - 2.0 * cross
    )


def combine_lse(left_pair, right_pair):
    left_max, left_sum = left_pair
    right_max, right_sum = right_pair
    joined = jnp.maximum(left_max, right_max)
    return (joined, left_sum * jnp.exp(left_max - joined) + right_sum * jnp.exp(right_max - joined))


def on_device(
    src_cent, tgt_cent, src_mass, tgt_mass, src_pts, tgt_pts, src_cluster, tgt_cluster, support
):
    coarse_cost = pair_cost(src_cent, tgt_cent)
    log_src = jnp.log(src_mass)
    log_tgt = jnp.log(tgt_mass)
    coarse_g = jnp.zeros(coarse_cost.shape[1], jnp.float32)
    coarse_f = jnp.zeros(coarse_cost.shape[0], jnp.float32)
    for turn_index in range(ITERS):
        scores = log_tgt[None, :] + (coarse_g[None, :] - coarse_cost) / EPS
        maxima = jnp.max(scores, 1)
        totals = jnp.sum(jnp.exp(scores - maxima[:, None]), 1)
        maxima, totals = combined_all((maxima, totals), "col", combine_lse)
        coarse_f = -EPS * (maxima + jnp.log(totals))
        scores = log_src[:, None] + (coarse_f[:, None] - coarse_cost) / EPS
        maxima = jnp.max(scores, 0)
        totals = jnp.sum(jnp.exp(scores - maxima[None, :]), 0)
        maxima, totals = combined_all((maxima, totals), "row", combine_lse)
        coarse_g = -EPS * (maxima + jnp.log(totals))
    all_f = lax.all_gather(coarse_f, "row", axis=0, tiled=True)
    all_g = lax.all_gather(coarse_g, "col", axis=0, tiled=True)
    start_f = jnp.take(all_f, src_cluster)
    start_g = jnp.take(all_g, tgt_cluster)
    devices = lax.axis_size(("row", "col"))
    requests_each = SB_DEV * SUPP
    slots_each = requests_each // devices + 1
    wanted = support.reshape(-1)
    owners = wanted // TB_DEV
    local_ids = wanted % TB_DEV
    positions = jnp.arange(requests_each, dtype=jnp.int32)
    earlier = (owners[None, :] == owners[:, None]) & (positions[None, :] < positions[:, None])
    occurs = jnp.sum(earlier.astype(jnp.int32), 1)
    slot_ids = owners * slots_each + occurs
    matches = slot_ids[None, :] == jnp.arange(devices * slots_each, dtype=jnp.int32)[:, None]
    table_ids = jnp.sum(jnp.where(matches, local_ids[None, :] + 1, 0), 1) - 1
    incoming = lax.all_to_all(
        table_ids.reshape(devices, slots_each),
        ("row", "col"),
        split_axis=0,
        concat_axis=0,
        tiled=True,
    )
    picked = jnp.maximum(incoming, 0).reshape(-1)
    send_pts = jnp.take(tgt_pts.reshape(F, TB_DEV, BLK), picked, axis=1)
    send_duals = jnp.take(start_g.reshape(TB_DEV, BLK), picked, axis=0)
    bundle = jnp.concatenate([send_pts, send_duals[None]], 0).reshape(
        F + 1, devices, slots_each, BLK
    )
    received = lax.all_to_all(bundle, ("row", "col"), split_axis=1, concat_axis=1, tiled=True)
    flat_recv = received.reshape(F + 1, devices * slots_each, BLK)
    tiles = jnp.take(flat_recv, slot_ids, axis=1).reshape(F + 1, SB_DEV, SUPP, BLK)

    def block_terms(block_index):
        start = block_index * BLK
        src_block = lax.dynamic_slice_in_dim(src_pts, start, BLK, 1)
        src_dual = lax.dynamic_slice_in_dim(start_f, start, BLK, 0)
        tile = lax.dynamic_slice_in_dim(tiles, block_index, 1, 1)[:, 0]
        tgt_sel = tile[:F]
        tgt_dual = tile[F]
        cross = jnp.einsum(
            "fi,fkj->ikj",
            src_block,
            tgt_sel,
            precision=lax.Precision.HIGHEST,
            preferred_element_type=jnp.float32,
        )
        distance = (
            jnp.sum(src_block * src_block, 0)[:, None, None]
            + jnp.sum(tgt_sel * tgt_sel, 0)[None, :, :]
            - 2.0 * cross
        )
        block_scores = (tgt_dual[None, :, :] - distance) / EPS
        row_max = jnp.max(block_scores, (1, 2))
        row_term = -EPS * (
            row_max
            + jnp.log(jnp.sum(jnp.exp(block_scores - row_max[:, None, None]), (1, 2)))
            - jnp.log(float(SUPP * BLK))
        )
        block_scores = (src_dual[:, None, None] - distance) / EPS
        part_max = jnp.max(block_scores, 0)
        part_sum = jnp.sum(jnp.exp(block_scores - part_max[None]), 0)
        return (row_term, part_max, part_sum)

    row_terms, part_max, part_sum = lax.map(block_terms, jnp.arange(SB_DEV, dtype=jnp.int32))
    match_float = matches.astype(jnp.float32)
    back_max = jnp.dot(
        match_float,
        part_max.reshape(requests_each, BLK),
        precision=lax.Precision.HIGHEST,
        preferred_element_type=jnp.float32,
    )
    back_sum = jnp.dot(
        match_float,
        part_sum.reshape(requests_each, BLK),
        precision=lax.Precision.HIGHEST,
        preferred_element_type=jnp.float32,
    )
    ret_max, ret_sum = (
        lax.all_to_all(
            back_max.reshape(devices, slots_each, BLK),
            ("row", "col"),
            split_axis=0,
            concat_axis=0,
            tiled=True,
        ),
        lax.all_to_all(
            back_sum.reshape(devices, slots_each, BLK),
            ("row", "col"),
            split_axis=0,
            concat_axis=0,
            tiled=True,
        ),
    )
    ret_max = ret_max.reshape(devices * slots_each, BLK)
    ret_sum = ret_sum.reshape(devices * slots_each, BLK)
    owner_mask = incoming.reshape(-1)[:, None] == jnp.arange(TB_DEV, dtype=jnp.int32)[None, :]
    col_max = jnp.max(jnp.where(owner_mask[:, :, None], ret_max[:, None, :], -jnp.inf), 0)
    col_sum = jnp.sum(
        jnp.where(
            owner_mask[:, :, None],
            ret_sum[:, None, :] * jnp.exp(ret_max[:, None, :] - col_max[None]),
            0.0,
        ),
        0,
    )
    named = jnp.sum(owner_mask.astype(jnp.float32), 0)
    col_term = -EPS * (col_max + jnp.log(col_sum) - jnp.log(named * BLK)[:, None])
    fine_f = 0.5 * (start_f + row_terms.reshape(-1))
    fine_g = 0.5 * (start_g + col_term.reshape(-1))
    return (coarse_f, coarse_g, fine_f, fine_g)


def solution(mesh):
    in_specs = (
        P(None, "row"),
        P(None, "col"),
        P("row"),
        P("col"),
        P(None, ("row", "col")),
        P(None, ("row", "col")),
        P(("row", "col")),
        P(("row", "col")),
        P(("row", "col"), None),
    )
    out_specs = (P("row"), P("col"), P(("row", "col")), P(("row", "col")))
    return jax.shard_map(
        on_device, mesh=mesh, in_specs=in_specs, out_specs=out_specs, check_vma=False
    )
```

profile of v0, /device:TPU:1, one launch (start us, length us, event | category | flops | bytes accessed | tf_op | source)
XLA Modules:
  0.0 879.2 jit_solution(5708205434779217815)
XLA Ops:
  2.5 11.5 %all-to-all-start = ((s32[128,1,2]{2,1,0:T(1,128)}), s32[128,1,2]{2,1,0:T(1,128)S(1)}, u32[]{:S(2)}, u32[]{:S(2)}) async-start(s32[128,1,2]{2,1,0:T(1,128)} %bitcast.86), calls=%async_computation | async-start | bytes 131072 | tf_op jit(solution)/shard_map/all_to_all | solution.py:84
  18.7 25.6 %all-gather.1 = f32[32768]{0:T(1024)S(1)} all-gather(f32[1024]{0:T(1024)S(1)} %exponential_reduce_fusion.17), channel_id=3, replica_groups=mesh['row'=4,'col'=32] {'col'}, dimensions={0}, use_global_device_ids=true | all-gather | bytes 135168 | tf_op jit(solution)/shard_map/all_gather | solution.py:18
  44.3 23.9 %all-gather = f32[32768]{0:T(1024)S(1)} all-gather(f32[1024]{0:T(1024)S(1)} %get-tuple-element.2505), channel_id=2, replica_groups=mesh['row'=4,'col'=32] {'col'}, dimensions={0}, use_global_device_ids=true | all-gather | bytes 135168 | tf_op jit(solution)/shard_map/all_gather | solution.py:18
  85.2 26.1 %all-gather.5 = f32[32768]{0:T(1024)S(1)} all-gather(f32[1024]{0:T(1024)S(1)} %exponential_reduce_fusion.15), channel_id=7, replica_groups=mesh['row'=4,'col'=32] {'col'}, dimensions={0}, use_global_device_ids=true | all-gather | bytes 135168 | tf_op jit(solution)/shard_map/all_gather | solution.py:18
  111.4 23.9 %all-gather.4 = f32[32768]{0:T(1024)S(1)} all-gather(f32[1024]{0:T(1024)S(1)} %fusion.24), channel_id=6, replica_groups=mesh['row'=4,'col'=32] {'col'}, dimensions={0}, use_global_device_ids=true | all-gather | bytes 135168 | tf_op jit(solution)/shard_map/all_gather | solution.py:18
  150.8 26.1 %all-gather.9 = f32[32768]{0:T(1024)S(1)} all-gather(f32[1024]{0:T(1024)S(1)} %exponential_reduce_fusion.13), channel_id=11, replica_groups=mesh['row'=4,'col'=32] {'col'}, dimensions={0}, use_global_device_ids=true | all-gather | bytes 135168 | tf_op jit(solution)/shard_map/all_gather | solution.py:18
  176.9 23.9 %all-gather.8 = f32[32768]{0:T(1024)S(1)} all-gather(f32[1024]{0:T(1024)S(1)} %fusion.26), channel_id=10, replica_groups=mesh['row'=4,'col'=32] {'col'}, dimensions={0}, use_global_device_ids=true | all-gather | bytes 135168 | tf_op jit(solution)/shard_map/all_gather | solution.py:18
  216.6 26.1 %all-gather.13 = f32[32768]{0:T(1024)S(1)} all-gather(f32[1024]{0:T(1024)S(1)} %exponential_reduce_fusion.11), channel_id=15, replica_groups=mesh['row'=4,'col'=32] {'col'}, dimensions={0}, use_global_device_ids=true | all-gather | bytes 135168 | tf_op jit(solution)/shard_map/all_gather | solution.py:18
  242.8 23.9 %all-gather.12 = f32[32768]{0:T(1024)S(1)} all-gather(f32[1024]{0:T(1024)S(1)} %fusion.28), channel_id=14, replica_groups=mesh['row'=4,'col'=32] {'col'}, dimensions={0}, use_global_device_ids=true | all-gather | bytes 135168 | tf_op jit(solution)/shard_map/all_gather | solution.py:18
  282.1 26.1 %all-gather.17 = f32[32768]{0:T(1024)S(1)} all-gather(f32[1024]{0:T(1024)S(1)} %exponential_reduce_fusion.9), channel_id=19, replica_groups=mesh['row'=4,'col'=32] {'col'}, dimensions={0}, use_global_device_ids=true | all-gather | bytes 135168 | tf_op jit(solution)/shard_map/all_gather | solution.py:18
  308.3 23.9 %all-gather.16 = f32[32768]{0:T(1024)S(1)} all-gather(f32[1024]{0:T(1024)S(1)} %fusion.30), channel_id=18, replica_groups=mesh['row'=4,'col'=32] {'col'}, dimensions={0}, use_global_device_ids=true | all-gather | bytes 135168 | tf_op jit(solution)/shard_map/all_gather | solution.py:18
  347.7 26.1 %all-gather.21 = f32[32768]{0:T(1024)S(1)} all-gather(f32[1024]{0:T(1024)S(1)} %exponential_reduce_fusion.7), channel_id=23, replica_groups=mesh['row'=4,'col'=32] {'col'}, dimensions={0}, use_global_device_ids=true | all-gather | bytes 135168 | tf_op jit(solution)/shard_map/all_gather | solution.py:18
  373.9 23.9 %all-gather.20 = f32[32768]{0:T(1024)S(1)} all-gather(f32[1024]{0:T(1024)S(1)} %fusion.32), channel_id=22, replica_groups=mesh['row'=4,'col'=32] {'col'}, dimensions={0}, use_global_device_ids=true | all-gather | bytes 135168 | tf_op jit(solution)/shard_map/all_gather | solution.py:18
  413.2 26.1 %all-gather.25 = f32[32768]{0:T(1024)S(1)} all-gather(f32[1024]{0:T(1024)S(1)} %exponential_reduce_fusion.5), channel_id=27, replica_groups=mesh['row'=4,'col'=32] {'col'}, dimensions={0}, use_global_device_ids=true | all-gather | bytes 135168 | tf_op jit(solution)/shard_map/all_gather | solution.py:18
  439.4 35.4 %all-gather.24 = f32[32768]{0:T(1024)S(1)} all-gather(f32[1024]{0:T(1024)S(1)} %fusion.34), channel_id=26, replica_groups=mesh['row'=4,'col'=32] {'col'}, dimensions={0}, use_global_device_ids=true | all-gather | bytes 135168 | tf_op jit(solution)/shard_map/all_gather | solution.py:18
  490.3 26.1 %all-gather.29 = f32[32768]{0:T(1024)S(1)} all-gather(f32[1024]{0:T(1024)S(1)} %exponential_reduce_fusion.3), channel_id=31, replica_groups=mesh['row'=4,'col'=32] {'col'}, dimensions={0}, use_global_device_ids=true | all-gather | bytes 135168 | tf_op jit(solution)/shard_map/all_gather | solution.py:18
  516.5 23.9 %all-gather.28 = f32[32768]{0:T(1024)S(1)} all-gather(f32[1024]{0:T(1024)S(1)} %fusion.36), channel_id=30, replica_groups=mesh['row'=4,'col'=32] {'col'}, dimensions={0}, use_global_device_ids=true | all-gather | bytes 135168 | tf_op jit(solution)/shard_map/all_gather | solution.py:18
  555.3 22.7 %all-gather.48 = f32[32,1,128]{2,1,0:T(1,128)S(1)} all-gather(f32[1,1,128]{2,1,0:T(1,128)S(1)} %bitcast.360), channel_id=1, replica_groups=mesh['row'=4,'col'=32] {'col'}, dimensions={0}, use_global_device_ids=true | all-gather | bytes 16896 | tf_op jit(solution)/shard_map/all_gather | solution.py:69
  578.0 45.5 %gather_fusion.2 = f32[8192]{0:T(1024)S(1)} fusion(f32[4096]{0:T(1024)S(1)} %bitcast.297, s32[8192]{0:T(1024)S(1)} %fusion.47), kind=kCustom, calls=%fused_computation.2 | custom fusion | bytes 98304 | tf_op jit(solution)/shard_map/jit(_take)/gather | solution.py:71
  648.9 52.1 %all_gather.262 = f32[4096]{0:T(1024)S(1)} all-gather(f32[1024]{0:T(1024)S(1)} %add_multiply_fusion.3), channel_id=1, replica_groups=mesh['row'=4,'col'=32] {'row'}, dimensions={0}, use_global_device_ids=true | all-gather | bytes 20480 | tf_op jit(solution)/shard_map/all_gather | solution.py:68
  701.0 11.8 %gather_fusion = f32[2048]{0:T(1024)S(1)} fusion(f32[4096]{0:T(1024)S(1)} %all_gather.262, s32[2048]{0:T(1024)S(1)} %fusion.48), kind=kCustom, calls=%fused_computation | custom fusion | bytes 24576 | tf_op jit(solution)/shard_map/jit(_take)/gather | solution.py:70
  724.6 109.1 %while.304 = (s32[]{:T(128)}, f32[8,256]{1,0:T(8,128)S(1)}, f32[8,16,256]{2,1,0:T(8,128)S(1)}, f32[8,16,256]{2,1,0:T(8,128)S(1)}, s32[8]{0:T(128)S(1)}, /*index=...) while((s32[]{:T(128)}, f32[8,256]{1,0:T(8,128)S(1)}, ...), condition=%wide.region_75.76_spmd, body=%wide.region_68.75_spmd.sunk | while | flops 219279376 | bytes 9206033 | solution.py:132
  834.9 13.4 %all-to-all-start.2 = ((f32[128,2,256]{2,1,0:T(2,128)}), f32[128,2,256]{2,1,0:T(2,128)S(1)}, u32[]{:S(2)}, u32[]{:S(2)}) async-start(f32[128,2,256]{2,1,0:T(2,128)} %copy.46), calls=%async_computation.2 | async-start | bytes 524288 | tf_op jit(solution)/shard_map/all_to_all | solution.py:147
  850.1 9.1 %all-to-all-done.2 = f32[128,2,256]{2,1,0:T(2,128)S(1)} async-done(((f32[128,2,256]{2,1,0:T(2,128)}), f32[128,2,256]{2,1,0:T(2,128)S(1)}, u32[]{:S(2)}, u32[]{:S(2)}) %all-to-all-start.2) | async-done | bytes 262176 | tf_op jit(solution)/shard_map/all_to_all | solution.py:147
  (814 shorter events, 285.6 us)
Async XLA Ops:
  2.5 621.2 %all-to-all-start = ((s32[128,1,2]{2,1,0:T(1,128)}), s32[128,1,2]{2,1,0:T(1,128)S(1)}, u32[]{:S(2)}, u32[]{:S(2)}) async-start(s32[128,1,2]{2,1,0:T(1,128)} %bitcast.86), calls=%async_computation | async-start | bytes 131072 | tf_op jit(solution)/shard_map/all_to_all | solution.py:84
  400.1 177.9 %copy-start.1 = (s32[8192]{0:T(1024)S(1)}, s32[8192]{0:T(1024)}, u32[]{:S(2)}) copy-start(s32[8192]{0:T(1024)} %param.50) | copy-start | bytes 98308
  542.3 106.6 %copy-start.2 = (f32[1024]{0:T(1024)}, f32[1024]{0:T(1024)S(1)}, u32[]{:S(2)}) copy-start(f32[1024]{0:T(1024)S(1)} %add_multiply_fusion.3) | copy-start | bytes 12292
  555.3 68.3 %copy-start.5 = (f32[128]{0:T(128)}, f32[128]{0:T(128)S(1)}, u32[]{:S(2)}) copy-start(f32[128]{0:T(128)S(1)} %add_multiply_fusion.11) | copy-start | bytes 1540
  578.0 45.6 %copy-start = (f32[16,8192]{1,0:T(8,128)S(1)}, f32[16,8192]{1,0:T(8,128)}, u32[]{:S(2)}) copy-start(f32[16,8192]{1,0:T(8,128)} %param.48) | copy-start | bytes 1572868
  641.7 7.0 copy-start.3
  641.7 59.3 %copy-start.4 = (s32[2048]{0:T(1024)S(1)}, s32[2048]{0:T(1024)}, u32[]{:S(2)}) copy-start(s32[2048]{0:T(1024)} %param.49) | copy-start | bytes 24580
  641.7 71.6 %all-to-all-start.1 = ((f32[17,128,2,256]{3,2,0,1:T(2,128)}), f32[17,128,2,256]{3,2,0,1:T(2,128)}, u32[]{:S(2)}, u32[]{:S(2)}) async-start(f32[17,128,2,256]{3,2,0,1:T(2,128)} %pad_maximum_fusion), calls=%async_computation.1 | async-start | bytes 8912896 | tf_op jit(solution)/shard_map/all_to_all | solution.py:97
  834.9 24.4 %all-to-all-start.2 = ((f32[128,2,256]{2,1,0:T(2,128)}), f32[128,2,256]{2,1,0:T(2,128)S(1)}, u32[]{:S(2)}, u32[]{:S(2)}) async-start(f32[128,2,256]{2,1,0:T(2,128)} %copy.46), calls=%async_computation.2 | async-start | bytes 524288 | tf_op jit(solution)/shard_map/all_to_all | solution.py:147
  859.2 15.5 %all-to-all-start.3 = ((f32[128,2,256]{2,1,0:T(2,128)}), f32[128,2,256]{2,1,0:T(2,128)S(1)}, u32[]{:S(2)}, u32[]{:S(2)}) async-start(f32[128,2,256]{2,1,0:T(2,128)} %copy.47), calls=%async_computation.3 | async-start | bytes 524288 | tf_op jit(solution)/shard_map/all_to_all | solution.py:154
where the time goes:
time: 890 us; the launch traced here: 879 us
  blocking collectives  584 us (66%)
  local copies, waits for them, and re-layouts  94.5 us (11%)
  other arithmetic  67.3 us (8%)
  matrix products  47.8 us (5%)
  starting transfers between devices  36.6 us (4%)
  loops' own time  29.7 us (3%)
  waiting for transfers between devices  17.5 us (2%)
    all_gather x32, blocking collectives, combined_all(): everything = jax.tree.map(lambda part: lax.all_gather(part, axis), x)  509 us
    all_gather x1, blocking collectives, on_device(): all_f = lax.all_gather(coarse_f, 'row', axis=0, tiled=True)  52.1 us
    gather x1, local copies, waits for them, and re-layouts, on_device(): start_g = jnp.take(all_g, tgt_cluster)  45.5 us
    dot_general x8, matrix products, block_terms(): jnp.einsum('fi,fkj->ikj', src_block, tgt_sel, precision=lax.Precision.HIG...  45.1 us
    all_gather x1, blocking collectives, on_device(): all_g = lax.all_gather(coarse_g, 'col', axis=0, tiled=True)  22.7 us
    another operation x1, loops' own time, on_device(): lax.map(block_terms, jnp.arange(SB_DEV, dtype=jnp.int32))  21.2 us
  transfers between devices with their start and end apart: 4, of which 2 were waited for; matrix products, arithmetic and copies ran while one was open for 10% of the time, Pallas kernels for 0%

commit v1 on v0

v1 whole, which is shorter than its diff:
```python
import math

import jax
import jax.numpy as jnp
from jax import lax
from jax.experimental import pallas as pl
from jax.experimental.pallas import tpu as pltpu
from jax.sharding import PartitionSpec as P

MESH = pl.DeviceIdType.MESH
F = 16
BLK = 256
SUPP = 16
SB_DEV = 8
TB_DEV = 32
KS = 4096
KT = 4096
EPS = 0.1
KAPPA = math.log2(math.e) / EPS
UNIT = EPS * math.log(2.0)
DEV = 128
HALF = KS // 2
CH = 64
NJ = KT // 128
VMEM = pl.BlockSpec(memory_space=pltpu.VMEM)
SMEM = pl.BlockSpec(memory_space=pltpu.SMEM)
f32 = jnp.float32
i32 = jnp.int32
bf16 = jnp.bfloat16


def split3(v):
    hi = v.astype(bf16)
    rest = v - hi.astype(f32)
    mid = rest.astype(bf16)
    return hi, mid, (rest - mid.astype(f32)).astype(bf16)


def stack(pts, term, left):
    h, m, l = split3(pts)
    n = pts.shape[1]
    th, tm, tl = [v.astype(f32) for v in split3(term)]
    rid = lax.broadcasted_iota(i32, (16, n), 0)
    base, ones = (0, 3) if left else (3, 0)
    extra = jnp.where(rid == base, th, jnp.where(rid == base + 1, tm, jnp.where(rid == base + 2, tl, 0.0)))
    extra = jnp.where((rid >= ones) & (rid < ones + 3), 1.0, extra).astype(bf16)
    zero = jnp.zeros((16, n), bf16)
    if left:
        return jnp.concatenate([h, h, m, h, l, m, extra, zero], 0)
    return jnp.concatenate([h, m, h, l, h, m, extra, zero], 0)


def left_rows(x):
    term = -KAPPA * jnp.sum(x * x, 0, keepdims=True)
    return stack((2.0 * KAPPA) * x, term, True).astype(f32).T.astype(bf16)


def spread(row):
    return jnp.broadcast_to(row, (128, 128)).T


def block(j, width=128):
    return slice(j * width, (j + 1) * width)


def gather_kernel(src_ref, smass_ref, tgt_ref, tmass_ref, src_out, smass_out, tgt_out, tmass_out, ssem, rsem, lsem):
    row = lax.axis_index("row")
    col = lax.axis_index("col")
    core = lax.rem(col, 2)
    peers = [({"row": lax.rem(row + d, 4), "col": col}, d) for d in range(1, 4)]
    cpeers = [({"row": row, "col": lax.rem(col + d, 32)}, d) for d in range(1, 32)]
    barrier = pltpu.get_barrier_semaphore()
    for peer, _ in peers + cpeers:
        pl.semaphore_signal(barrier, inc=1, device_id=peer, device_id_type=MESH)
    pl.semaphore_wait(barrier, 34)
    half = pl.ds(pl.multiple_of(core * 512, 512), 512)
    copies = []
    for n, (peer, d) in enumerate(cpeers):
        for a, (src, dst) in enumerate(((tgt_ref, tgt_out), (tmass_ref, tmass_out))):
            copies.append(pltpu.make_async_remote_copy(
                src_ref=src, dst_ref=dst.at[col], send_sem=ssem.at[n, a], recv_sem=rsem.at[n, a],
                device_id=peer, device_id_type=MESH))
    for n, (peer, d) in enumerate(peers):
        for a, (src, dst) in enumerate(((src_ref, src_out), (smass_ref, smass_out))):
            copies.append(pltpu.make_async_remote_copy(
                src_ref=src.at[:, half], dst_ref=dst.at[row], send_sem=ssem.at[31 + n, a],
                recv_sem=rsem.at[31 + n, a], device_id=peer, device_id_type=MESH))
    for c in copies:
        c.start()
    local = [pltpu.make_async_copy(tgt_ref, tgt_out.at[col], lsem.at[0]),
             pltpu.make_async_copy(tmass_ref, tmass_out.at[col], lsem.at[1]),
             pltpu.make_async_copy(src_ref.at[:, half], src_out.at[row], lsem.at[2]),
             pltpu.make_async_copy(smass_ref.at[:, half], smass_out.at[row], lsem.at[3])]
    for c in local:
        c.start()
    for c in local + copies:
        c.wait()


def gather_centroids(src_cent, src_mass, tgt_cent, tgt_mass):
    return pl.pallas_call(
        gather_kernel,
        out_shape=(jax.ShapeDtypeStruct((4, F, 512), f32), jax.ShapeDtypeStruct((4, 1, 512), f32),
                   jax.ShapeDtypeStruct((32, F, 128), f32), jax.ShapeDtypeStruct((32, 1, 128), f32)),
        in_specs=[VMEM] * 4,
        out_specs=(VMEM,) * 4,
        scratch_shapes=[pltpu.SemaphoreType.DMA((34, 2)), pltpu.SemaphoreType.DMA((34, 2)),
                        pltpu.SemaphoreType.DMA((4,))],
        compiler_params=pltpu.CompilerParams(collective_id=0, has_side_effects=True),
        name="gather_centroids",
    )(src_cent, src_mass.reshape(1, -1), tgt_cent, tgt_mass.reshape(1, -1))


def sinkhorn_kernel(src_ref, smass_ref, tgt_ref, tmass_ref, ftab_ref, gtab_ref,
                    a_scr, d0, d1, t0, t1, ys, xs, gp, lb, acc, fst, am, sbuf, rbuf, fs_buf, fr_buf,
                    send_sem, recv_sem, fsend, frecv):
    row = lax.axis_index("row")
    col = lax.axis_index("col")
    core = lax.rem(col, 2)
    partner = {"row": row, "col": col + 1 - 2 * core}
    barrier = pltpu.get_barrier_semaphore()
    pl.semaphore_signal(barrier, inc=1, device_id=partner, device_id_type=MESH)
    pl.semaphore_wait(barrier, 1)
    for k in range(32):
        y = tgt_ref[k]
        lbk = jnp.log2(tmass_ref[k])
        ys[:, block(k)] = stack(y, lbk - KAPPA * jnp.sum(y * y, 0, keepdims=True), False)
        lb[:, block(k)] = jnp.broadcast_to(lbk, (8, 128))
    for q in range(4):
        for h in range(4):
            r0 = q * 512 + h * 128
            xs[r0:r0 + 128, :] = left_rows(src_ref[q, :, block(h)])
            am[r0:r0 + 128, :] = spread(smass_ref[q, :, block(h)])
    acc[...] = jnp.full_like(acc, -jnp.inf)

    def product(dst, b, quarter):
        xc = xs[pl.ds(pl.multiple_of(b * 256, 256), 256), :]
        for u in range(2):
            c0 = quarter * 1024 + u * 512
            dst[:, c0:c0 + 512] = jnp.dot(xc, ys[:, c0:c0 + 512], preferred_element_type=f32)

    def first(src, b, quarter):
        rr = block(quarter, CH)
        mx = src[rr, block(0)]
        for j in range(1, NJ):
            mx = jnp.maximum(mx, src[rr, block(j)])
        mx = jnp.broadcast_to(jnp.max(mx, 1, keepdims=True), (CH, 128))
        s = jnp.exp2(src[rr, block(0)] - mx)
        for j in range(1, NJ):
            s = s + jnp.exp2(src[rr, block(j)] - mx)
        s = jnp.broadcast_to(jnp.sum(s, 1, keepdims=True), (CH, 128))
        f1 = -(mx + jnp.log2(s))
        rows = pl.ds(pl.multiple_of(b * 256 + quarter * CH, CH), CH)
        fst[rows, :] = f1
        fl = f1 + jnp.log2(am[rows, :])
        for j in range(NJ):
            v = src[rr, block(j)] + fl
            a_scr[rows, block(j)] = v
            acc[:, block(j)] = jnp.maximum(acc[:, block(j)], jnp.max(v.reshape(CH // 8, 8, 128), 0))

    for quarter in range(4):
        product(d0, 0, quarter)

    def pair(p, _):
        for quarter in range(4):
            product(d1, 2 * p + 1, quarter)
            first(d0, 2 * p, quarter)
        for quarter in range(4):
            product(d0, lax.rem(2 * p + 2, 8), quarter)
            first(d1, 2 * p + 1, quarter)
        return 0

    lax.fori_loop(0, 4, pair, 0)
    for j in range(NJ):
        gp[:, block(j)] = jnp.broadcast_to(jnp.max(acc[:, block(j)], 0, keepdims=True), (8, 128))
    acc[...] = jnp.zeros_like(acc)

    def second(c, _):
        rows = pl.ds(pl.multiple_of(c * CH, CH), CH)
        for j in range(NJ):
            v = a_scr[rows, block(j)].reshape(CH // 8, 8, 128) - gp[:, block(j)][None]
            acc[:, block(j)] = acc[:, block(j)] + jnp.sum(jnp.exp2(v), 0)
        return 0

    lax.fori_loop(0, HALF // CH, second, 0)
    for j in range(NJ):
        sbuf[0, :, block(j)] = gp[:1, block(j)] + jnp.log2(jnp.sum(acc[:, block(j)], 0, keepdims=True))

    def swap(k):
        cp = pltpu.make_async_remote_copy(src_ref=sbuf.at[k], dst_ref=rbuf.at[k], send_sem=send_sem.at[k],
                                          recv_sem=recv_sem.at[k], device_id=partner, device_id_type=MESH)
        cp.start()
        cp.wait()

    swap(0)
    for j in range(NJ):
        l0, l1 = sbuf[0, :, block(j)], rbuf[0, :, block(j)]
        m = jnp.maximum(l0, l1)
        l = m + jnp.log2(jnp.exp2(l0 - m) + jnp.exp2(l1 - m))
        gp[:, block(j)] = lb[:, block(j)] - jnp.broadcast_to(l, (8, 128))

    def turn(k, restab, last):
        acc[...] = jnp.zeros_like(acc)

        def scores(t, rows):
            r = None
            for j in range(NJ):
                v = a_scr[rows, block(j)].reshape(CH // 8, 8, 128) + gp[:, block(j)][None]
                e = jnp.exp2(v).reshape(CH, 128)
                t[:, block(j)] = e
                r = e if r is None else r + e
            return jnp.broadcast_to(jnp.sum(r, 1, keepdims=True), (CH, 128))

        def sums(t, rows, r):
            u = am[rows, :] / r
            if restab or last:
                step = -jnp.log2(u)
                fst[rows, :] = fst[rows, :] - step
            for j in range(NJ):
                acc[:, block(j)] = acc[:, block(j)] + jnp.sum((t[:, block(j)] * u).reshape(CH // 8, 8, 128), 0)
                if restab:
                    a_scr[rows, block(j)] = a_scr[rows, block(j)] - step

        def chunk(c, _):
            ra = pl.ds(pl.multiple_of(c * 2 * CH, CH), CH)
            rb = pl.ds(pl.multiple_of(c * 2 * CH + CH, CH), CH)
            sa = scores(t0, ra)
            sb = scores(t1, rb)
            sums(t0, ra, sa)
            sums(t1, rb, sb)
            return 0

        lax.fori_loop(0, HALF // CH // 2, chunk, 0)
        for j in range(NJ):
            sbuf[k, :, block(j)] = jnp.sum(acc[:, block(j)], 0, keepdims=True)
        swap(k)
        for j in range(NJ):
            c = jnp.broadcast_to(sbuf[k, :, block(j)] + rbuf[k, :, block(j)], (8, 128))
            gp[:, block(j)] = gp[:, block(j)] + (lb[:, block(j)] - jnp.log2(c))

    def two(p, _):
        turn(2 * p + 1, False, False)
        turn(2 * p + 2, True, False)
        return 0

    lax.fori_loop(0, 3, two, 0)
    turn(7, False, True)
    for h in range(16):
        fs_buf[h:h + 1, :] = (fst[block(h), :] * UNIT).T[:1, :]
    cp = pltpu.make_async_remote_copy(src_ref=fs_buf, dst_ref=fr_buf, send_sem=fsend, recv_sem=frecv,
                                      device_id=partner, device_id_type=MESH)
    cp.start()
    for j in range(NJ):
        gtab_ref[j:j + 1, :] = gp[:1, block(j)] * UNIT
    cp.wait()
    for q in range(4):
        a, b = fs_buf[q * 4:q * 4 + 4], fr_buf[q * 4:q * 4 + 4]
        ftab_ref[q * 8:q * 8 + 4, :] = jnp.where(core == 0, a, b)
        ftab_ref[q * 8 + 4:q * 8 + 8, :] = jnp.where(core == 0, b, a)


def sinkhorn(src_all, smass_all, tgt_all, tmass_all):
    V = pltpu.VMEM
    dma = pltpu.SemaphoreType.DMA
    return pl.pallas_call(
        sinkhorn_kernel,
        out_shape=(jax.ShapeDtypeStruct((32, 128), f32), jax.ShapeDtypeStruct((32, 128), f32)),
        in_specs=[VMEM] * 4,
        out_specs=(VMEM, VMEM),
        scratch_shapes=[V((HALF, KT), f32), V((256, KT), f32), V((256, KT), f32), V((CH, KT), f32), V((CH, KT), f32),
                        V((128, KT), bf16), V((HALF, 128), bf16), V((8, KT), f32), V((8, KT), f32), V((8, KT), f32),
                        V((HALF, 128), f32), V((HALF, 128), f32), V((8, 1, KT), f32), V((8, 1, KT), f32),
                        V((16, 128), f32), V((16, 128), f32), dma((8,)), dma((8,)), dma, dma],
        compiler_params=pltpu.CompilerParams(collective_id=1, has_side_effects=True,
                                             vmem_limit_bytes=60 * 1024 * 1024),
        cost_estimate=pl.CostEstimate(flops=60_000_000_000, bytes_accessed=1 << 20, transcendentals=1 << 26),
        name="sinkhorn",
    )(src_all, smass_all, tgt_all, tmass_all)


def request_kernel(sup_ref, req_ref, slot_ref):
    wanted = sup_ref[...].astype(f32)
    owner = jnp.floor(wanted * (1.0 / TB_DEV))
    local = wanted - owner * TB_DEV
    sub = lax.broadcasted_iota(i32, (128, 128), 0)
    lane = lax.broadcasted_iota(i32, (128, 128), 1)
    lanef = lane.astype(f32)
    same = jnp.broadcast_to(owner, (128, 128)) == sub.astype(f32)
    lo = jnp.min(jnp.where(same, lanef, 1e6), 1, keepdims=True)
    hi = jnp.max(jnp.where(same, lanef, -1.0), 1, keepdims=True)
    locb = jnp.broadcast_to(local, (128, 128)) + 1.0
    id0 = jnp.sum(jnp.where(lanef == lo, locb, 0.0), 1, keepdims=True) - 1.0
    id1 = jnp.sum(jnp.where((lanef == hi) & (hi > lo), locb, 0.0), 1, keepdims=True) - 1.0
    req_ref[...] = jnp.where(lane == 0, id0, jnp.where(lane == 1, id1, 0.0)).astype(i32)
    ownc = spread(owner)
    before = jnp.where((ownc == jnp.broadcast_to(owner, (128, 128))) & (sub < lane), 1.0, 0.0)
    slot_ref[...] = (owner * 2.0 + jnp.sum(before, 0, keepdims=True)).astype(i32)


def make_requests(support):
    return pl.pallas_call(
        request_kernel,
        out_shape=(jax.ShapeDtypeStruct((128, 128), i32), jax.ShapeDtypeStruct((1, 128), i32)),
        in_specs=[VMEM], out_specs=(VMEM, VMEM), name="make_requests",
    )(support.reshape(1, 128))


def pick_kernel(inc_ref, pts_ref, clu_ref, pts_out, clu_out):
    def one(p, _):
        for q in range(2):
            t = jnp.maximum(inc_ref[p, q], 0)
            pts_out[p, q] = pts_ref[:, pl.ds(pl.multiple_of(t * BLK, BLK), BLK)]
            clu_out[p, 2 * q:2 * q + 2, :] = clu_ref[t]
        return 0

    lax.fori_loop(0, DEV, one, 0)


def pick(incoming, tgt_pts, tgt_cluster):
    return pl.pallas_call(
        pick_kernel,
        out_shape=(jax.ShapeDtypeStruct((DEV, 2, F, BLK), f32), jax.ShapeDtypeStruct((DEV, 4, 128), i32)),
        in_specs=[SMEM, VMEM, VMEM], out_specs=(VMEM, VMEM), name="pick",
    )(incoming, tgt_pts, tgt_cluster.reshape(TB_DEV, 2, 128))


def lookup(tab, idx):
    low = idx & 127
    high = idx >> 7
    out = jnp.zeros((8, 128), f32)
    for r in range(32):
        got = jnp.take_along_axis(jnp.broadcast_to(tab[r:r + 1, :], (8, 128)), low, axis=1)
        out = jnp.where(high == r, got, out)
    return out


def fine_kernel(slot_ref, ftab_ref, gtab_ref, src_ref, sclu_ref, tgt_ref, tclu_ref, oclu_ref,
                cf_ref, cg_ref, ff_ref, sg_ref, back_ref, gs, fs, xt, fx, sc, rm):
    row = lax.axis_index("row")
    col = lax.axis_index("col")
    cf_ref[...] = ftab_ref[pl.ds(pl.multiple_of(row * 8, 8), 8), :]
    cg_ref[...] = gtab_ref[pl.ds(col, 1), :]
    ft = ftab_ref[...] * KAPPA
    gt = gtab_ref[...] * KAPPA
    for r in range(2):
        fs[block(r, 8), :] = lookup(ft, sclu_ref[block(r, 8), :])

    def own(r, _):
        rows = pl.ds(pl.multiple_of(r * 8, 8), 8)
        sg_ref[rows, :] = lookup(gt, oclu_ref[rows, :]) * UNIT
        return 0

    lax.fori_loop(0, 8, own, 0)

    def sent(r, _):
        rows = pl.ds(pl.multiple_of(r * 8, 8), 8)
        gs[rows, :] = lookup(gt, tclu_ref[rows, :])
        return 0

    lax.fori_loop(0, 64, sent, 0)

    def one_block(b, _):
        for h in range(2):
            cols = pl.ds(pl.multiple_of(b * BLK + h * 128, 128), 128)
            xt[block(h), :] = left_rows(src_ref[:, cols])
            fx[block(h), :] = spread(fs[pl.ds(2 * b + h, 1), :])
        rm[...] = jnp.full_like(rm, -jnp.inf)

        def some(g, _):
            for u in range(2):
                k = 2 * g + u
                slot = slot_ref[b * SUPP + k]
                y = tgt_ref[slot]
                gj = jnp.concatenate([gs[pl.ds(2 * slot, 1), :], gs[pl.ds(2 * slot + 1, 1), :]], 1)
                st = stack(y, gj - KAPPA * jnp.sum(y * y, 0, keepdims=True), False)
                d = jnp.dot(xt[...], st, preferred_element_type=f32)
                sc[k] = d
                rm[...] = jnp.maximum(rm[...], jnp.maximum(d[:, :128], d[:, 128:]))
                for h in range(2):
                    v = d[:, block(h)] + fx[...]
                    m = jnp.max(v, 0, keepdims=True)
                    s = jnp.sum(jnp.exp2(v - m), 0, keepdims=True)
                    back_ref[pl.ds(2 * slot + h, 1), :] = m + jnp.log2(s) - gj[:, block(h)]
            return 0

        lax.fori_loop(0, SUPP // 2, some, 0)
        m = jnp.broadcast_to(jnp.max(rm[...], 1, keepdims=True), (BLK, 128))
        rm[...] = m

        def total(k, s):
            d = sc[k]
            return s + jnp.exp2(d[:, :128] - rm[...]) + jnp.exp2(d[:, 128:] - rm[...])

        s = lax.fori_loop(0, SUPP, total, jnp.zeros((BLK, 128), f32))
        lse = rm[...] + jnp.log2(jnp.sum(s, 1, keepdims=True)) - math.log2(SUPP * BLK)
        out = (0.5 * UNIT) * (fx[...] - lse)
        for h in range(2):
            ff_ref[pl.ds(2 * b + h, 1), :] = out[block(h), :].T[:1, :]
        return 0

    lax.fori_loop(0, SB_DEV, one_block, 0)


def fine(slots, ftab, gtab, src_pts, src_cluster, tiles, tclu, tgt_cluster):
    S = jax.ShapeDtypeStruct
    V = pltpu.VMEM
    return pl.pallas_call(
        fine_kernel,
        out_shape=(S((8, 128), f32), S((1, 128), f32), S((16, 128), f32), S((64, 128), f32), S((4 * DEV, 128), f32)),
        in_specs=[SMEM] + [VMEM] * 7,
        out_specs=(VMEM,) * 5,
        scratch_shapes=[V((4 * DEV, 128), f32), V((16, 128), f32), V((BLK, 128), bf16), V((BLK, 128), f32),
                        V((SUPP, BLK, BLK), f32), V((BLK, 128), f32)],
        name="fine",
    )(slots, ftab, gtab, src_pts, src_cluster.reshape(16, 128), tiles, tclu, tgt_cluster.reshape(64, 128))


def column_kernel(inc_ref, ret_ref, sg_ref, fg_ref, idr):
    for q in range(2):
        idr[q] = jnp.broadcast_to(inc_ref[:, q:q + 1].astype(f32), (DEV, 128))

    def one(t, _):
        tf = t.astype(f32)
        masks = [idr[q] == tf for q in range(2)]
        count = sum(jnp.sum(jnp.where(m, 1.0, 0.0), 0, keepdims=True) for m in masks)
        for h in range(2):
            vs = [ret_ref[pl.ds(2 * q + h, DEV, stride=4), :] for q in range(2)]
            m = [jnp.max(jnp.where(masks[q], vs[q], -jnp.inf), 0, keepdims=True) for q in range(2)]
            m = jnp.maximum(m[0], m[1])
            s = sum(jnp.sum(jnp.where(masks[q], jnp.exp2(vs[q] - m), 0.0), 0, keepdims=True) for q in range(2))
            lse = m + jnp.log2(s) - jnp.log2(count * BLK)
            fg_ref[pl.ds(2 * t + h, 1), :] = 0.5 * (sg_ref[pl.ds(2 * t + h, 1), :] - UNIT * lse)
        return 0

    lax.fori_loop(0, TB_DEV, one, 0)


def columns(incoming, ret, start_g):
    return pl.pallas_call(
        column_kernel,
        out_shape=jax.ShapeDtypeStruct((64, 128), f32),
        in_specs=[VMEM] * 3, out_specs=VMEM,
        scratch_shapes=[pltpu.VMEM((2, DEV, 128), f32)],
        name="columns",
    )(incoming, ret, start_g)


def exchange(x):
    return lax.all_to_all(x, ("row", "col"), split_axis=0, concat_axis=0, tiled=True)


def on_device(src_cent, tgt_cent, src_mass, tgt_mass, src_pts, tgt_pts, src_cluster, tgt_cluster, support):
    req, slots = make_requests(support)
    incoming = exchange(req)
    send_pts, send_clu = pick(incoming, tgt_pts, tgt_cluster)
    tiles = exchange(send_pts)
    tclu = exchange(send_clu)
    ftab, gtab = sinkhorn(*gather_centroids(src_cent, src_mass, tgt_cent, tgt_mass))
    cf, cg, ff, sg, back = fine(slots.reshape(128), ftab, gtab, src_pts, src_cluster,
                                tiles.reshape(2 * DEV, F, BLK), tclu.reshape(4 * DEV, 128), tgt_cluster)
    ret = exchange(back.reshape(DEV, 4, 128)).reshape(4 * DEV, 128)
    fg = columns(incoming, ret, sg)
    return cf.reshape(-1), cg.reshape(-1), ff.reshape(-1), fg.reshape(-1)


def solution(mesh):
    both = ("row", "col")
    in_specs = (P(None, "row"), P(None, "col"), P("row"), P("col"), P(None, both), P(None, both), P(both), P(both),
                P(both, None))
    out_specs = (P("row"), P("col"), P(both), P(both))
    return jax.shard_map(on_device, mesh=mesh, in_specs=in_specs, out_specs=out_specs, check_vma=False)
```

time: 890 us -> 213 us (0.24); the launches traced: 879 us -> 213 us
  blocking collectives: 584 us -> 41.2 us
  Pallas kernels: 0 us -> 156 us
  local copies, waits for them, and re-layouts: 94.5 us -> 2.01 us
  other arithmetic: 67.3 us -> 0 us
  matrix products: 47.8 us -> 0 us
  loops' own time: 29.7 us -> 0 us
  starting transfers between devices: 36.6 us -> 12.7 us
  waiting for transfers between devices: 17.5 us -> 0.01 us
    all_gather x34 -> x0, blocking collectives: 584 us -> none  [the longest x32 509 us: combined_all(): everything = jax.tree.map(lambda part: lax.all_gather(part, axis), x)]
    pallas_call x0 -> x6, Pallas kernels: none -> 156 us  [the longest x1 85.8 us: sinkhorn(): pl.pallas_call(sinkhorn_kernel, out_shape=(jax.ShapeDtypeStruct((32, 128)...]
    gather x6 -> x0, local copies, waits for them, and re-layouts: 64.9 us -> none  [the longest x1 45.5 us: on_device(): start_g = jnp.take(all_g, tgt_cluster)]
    dot_general x11 -> x0, matrix products: 47.8 us -> none  [the longest x8 45.1 us: block_terms(): jnp.einsum('fi,fkj->ikj', src_block, tgt_sel, precision=lax.Precision.HIG...]
    all_to_all x0 -> x2, blocking collectives: none -> 41.2 us  [exchange(): lax.all_to_all(x, ('row', 'col'), split_axis=0, concat_axis=0, tiled=True)]
    reduce_sum x46 -> x0, other arithmetic: 40.6 us -> none  [the longest x8 15.6 us: block_terms(): part_sum = jnp.sum(jnp.exp(block_scores - part_max[None]), 0)]
    another operation x17 -> x0, loops' own time: 29.7 us -> none  [the longest x1 21.2 us: on_device(): lax.map(block_terms, jnp.arange(SB_DEV, dtype=jnp.int32))]
    all_to_all x4 -> x2, starting transfers between devices: 36.6 us -> 12.7 us  [exchange(): lax.all_to_all(x, ('row', 'col'), split_axis=0, concat_axis=0, tiled=True)]
  transfers between devices with their start and end apart: 4 -> 2, of which waited for: 2 -> 0; matrix products, arithmetic and copies ran while one was open for 10% -> 0% of each run, Pallas kernels for 0% -> 47%
where the time goes in v1:
time: 213 us
  Pallas kernels  156 us (73%)
  blocking collectives  41.2 us (19%)
  starting transfers between devices  12.7 us (6%)
    pallas_call x1, Pallas kernels, sinkhorn(): pl.pallas_call(sinkhorn_kernel, out_shape=(jax.ShapeDtypeStruct((32, 128)...  85.8 us
    pallas_call x1, Pallas kernels, fine(): pl.pallas_call(fine_kernel, out_shape=(S((8, 128), f32), S((1, 128), f32)...  43 us
    all_to_all x2, blocking collectives, exchange(): lax.all_to_all(x, ('row', 'col'), split_axis=0, concat_axis=0, tiled=True)  41.2 us
    pallas_call x1, Pallas kernels, gather_centroids(): pl.pallas_call(gather_kernel, out_shape=(jax.ShapeDtypeStruct((4, F, 512)...  15.1 us
    all_to_all x2, starting transfers between devices, exchange(): lax.all_to_all(x, ('row', 'col'), split_axis=0, concat_axis=0, tiled=True)  12.7 us
    pallas_call x1, Pallas kernels, pick(): pl.pallas_call(pick_kernel, out_shape=(jax.ShapeDtypeStruct((DEV, 2, F, B...  5.37 us
    pallas_call x1, Pallas kernels, columns(): pl.pallas_call(column_kernel, out_shape=jax.ShapeDtypeStruct((64, 128), f...  5.35 us
  transfers between devices with their start and end apart: 2, of which 0 were waited for; matrix products, arithmetic and copies ran while one was open for 0% of the time, Pallas kernels for 47%

profile of v1, /device:TPU:1, one launch (start us, length us, event | category | flops | bytes accessed | tf_op | source)
XLA Modules:
  0.0 212.6 jit_solution(18302903384600601354)
XLA Ops:
  0.6 1.3 reshape.55.sup_ref
  1.9 1.5 make_requests.1
  3.4 21.2 %all_to_all.26 = s32[128,1,128]{2,1,0:T(1,128)} all-to-all(s32[128,1,128]{2,1,0:T(1,128)} %bitcast.25), channel_id=1, replica_groups=mesh['row'=4,'col'=32] {'row','col'}, dimensions={0} | all-to-all | bytes 131072 | tf_op jit(solution)/shard_map/all_to_all | solution.py:449
  24.6 5.4 %pick.1 = (f32[128,2,16,256]{3,2,1,0:T(8,128)}, s32[128,4,128]{2,1,0:T(4,128)}) custom-call(s32[128,128]{1,0:T(8,128)} %bitcast.20, f32[16,8192]{1,0:T(8,128)} %pts_ref.1, s32[32,2,128]{2,1,0:T(2,128)} %bitcast.23), custom_call_target="tpu_custom_call" | custom-call | tf_op jit(solution)/shard_map/pick/pallas_call | solution.py:320
  30.0 4.8 %all-to-all-start.2 = ((s32[128,4,128]{2,1,0:T(4,128)}), s32[128,4,128]{2,1,0:T(4,128)S(1)}, u32[]{:S(2)}, u32[]{:S(2)}) async-start(s32[128,4,128]{2,1,0:T(4,128)} %get-tuple-element.28), calls=%async_computation.2 | async-start | bytes 524288 | tf_op jit(solution)/shard_map/all_to_all | solution.py:449
  34.8 15.1 %gather_centroids.1 = (f32[4,16,512]{2,1,0:T(8,128)}, f32[4,1,512]{2,1,0:T(1,128)}, f32[32,16,128]{2,1,0:T(8,128)}, f32[32,1,128]{2,1,0:T(1,128)}) custom-call(f32[16,1024]{1,0:T(8,128)} %src_ref.2, f32[1,1024]{1,0:T(1,128)} %bitcast.28, f32[16,128]{1,0:T(8,128)} %tgt_ref.1, f32[1,128]{1,0:T(1,128)} %bitcast.29), custom_call_target="tpu_custom_call" | custom-call | tf_op jit(solution)/shard_map/gather_centroids/pallas_call | solution.py:101
  49.9 0.0 all-to-all-done.2
  49.9 0.0 copy-start
  49.9 0.7 copy-done
  50.6 7.9 %all-to-all-start.1 = ((f32[128,2,16,256]{3,2,1,0:T(8,128)}), f32[128,2,16,256]{3,2,1,0:T(8,128)}, u32[]{:S(2)}, u32[]{:S(2)}) async-start(f32[128,2,16,256]{3,2,1,0:T(8,128)} %get-tuple-element.27), calls=%async_computation.1 | async-start | bytes 8388608 | tf_op jit(solution)/shard_map/all_to_all | solution.py:449
  58.5 85.8 %sinkhorn.1 = (f32[32,128]{1,0:T(8,128)}, f32[32,128]{1,0:T(8,128)}) custom-call(f32[4,16,512]{2,1,0:T(8,128)} %get-tuple-element.20.src_ref, f32[4,1,512]{2,1,0:T(1,128)} %get-tuple-element.21.smass_ref, f32[32,16,128]{2,1,0:T(8,128)} %get-tuple-element.22.tgt_ref, f32[32,1,128]{2,1,0:T(1,128)} %get-tuple-element.23.tmass_ref), custom_call_target="tpu_custom_call" | custom-call | flops 60000002048 | bytes 1048576 | tf_op jit(solution)/shard_map/sinkhorn/pallas_call | solution.py:265
  144.3 0.0 all-to-all-done.1
  144.3 43.0 %fine.1 = (f32[8,128]{1,0:T(8,128)}, f32[1,128]{1,0:T(1,128)}, f32[16,128]{1,0:T(8,128)}, f32[64,128]{1,0:T(8,128)}, f32[512,128]{1,0:T(8,128)}) custom-call(s32[128]{0:T(128)} %bitcast.30, f32[32,128]{1,0:T(8,128)} %get-tuple-element.24.ftab_ref, f32[32,128]{1,0:T(8,128)} %get-tuple-element.25.gtab_ref, f32[16,2048]{1,0:T(8,128)} %src_ref.3, ...), custom_call_target="tpu_custom_call" | custom-call | tf_op jit(solution)/shard_map/fine/pallas_call | solution.py:407
  187.2 20.0 %all_to_all.27 = f32[128,4,128]{2,1,0:T(4,128)} all-to-all(f32[128,4,128]{2,1,0:T(4,128)} %bitcast.22), channel_id=1, replica_groups=mesh['row'=4,'col'=32] {'row','col'}, dimensions={0} | all-to-all | bytes 524288 | tf_op jit(solution)/shard_map/all_to_all | solution.py:449
  207.2 5.4 %columns.1 = f32[64,128]{1,0:T(8,128)} custom-call(s32[128,128]{1,0:T(8,128)} %bitcast.21, f32[512,128]{1,0:T(8,128)} %bitcast.19, f32[64,128]{1,0:T(8,128)} %get-tuple-element.33.sg_ref), custom_call_target="tpu_custom_call" | custom-call | tf_op jit(solution)/shard_map/columns/pallas_call | solution.py:439
Async XLA Ops:
  30.0 19.9 %all-to-all-start.2 = ((s32[128,4,128]{2,1,0:T(4,128)}), s32[128,4,128]{2,1,0:T(4,128)S(1)}, u32[]{:S(2)}, u32[]{:S(2)}) async-start(s32[128,4,128]{2,1,0:T(4,128)} %get-tuple-element.28), calls=%async_computation.2 | async-start | bytes 524288 | tf_op jit(solution)/shard_map/all_to_all | solution.py:449
  49.9 0.7 copy-start
  50.6 93.6 %all-to-all-start.1 = ((f32[128,2,16,256]{3,2,1,0:T(8,128)}), f32[128,2,16,256]{3,2,1,0:T(8,128)}, u32[]{:S(2)}, u32[]{:S(2)}) async-start(f32[128,2,16,256]{3,2,1,0:T(8,128)} %get-tuple-element.27), calls=%async_computation.1 | async-start | bytes 8388608 | tf_op jit(solution)/shard_map/all_to_all | solution.py:449

commit v2 on v1

v2 whole, which is shorter than its diff:
```python
import math

import jax
import jax.numpy as jnp
from jax import lax
from jax.experimental import pallas as pl
from jax.experimental.pallas import tpu as pltpu
from jax.sharding import PartitionSpec as P

MESH = pl.DeviceIdType.MESH
F = 16
BLK = 256
SUPP = 16
SB_DEV = 8
TB_DEV = 32
KS = 4096
KT = 4096
EPS = 0.1
KAPPA = math.log2(math.e) / EPS
UNIT = EPS * math.log(2.0)
DEV = 128
HALF = KS // 2
CH = 64
NJ = KT // 128
VMEM = pl.BlockSpec(memory_space=pltpu.VMEM)
SMEM = pl.BlockSpec(memory_space=pltpu.SMEM)
f32 = jnp.float32
i32 = jnp.int32
bf16 = jnp.bfloat16


def split3(v):
    hi = v.astype(bf16)
    rest = v - hi.astype(f32)
    mid = rest.astype(bf16)
    return hi, mid, (rest - mid.astype(f32)).astype(bf16)


def stack(pts, term, left):
    h, m, l = split3(pts)
    n = pts.shape[1]
    th, tm, tl = [v.astype(f32) for v in split3(term)]
    rid = lax.broadcasted_iota(i32, (16, n), 0)
    base, ones = (0, 3) if left else (3, 0)
    extra = jnp.where(rid == base, th, jnp.where(rid == base + 1, tm, jnp.where(rid == base + 2, tl, 0.0)))
    extra = jnp.where((rid >= ones) & (rid < ones + 3), 1.0, extra).astype(bf16)
    zero = jnp.zeros((16, n), bf16)
    if left:
        return jnp.concatenate([h, h, m, h, l, m, extra, zero], 0)
    return jnp.concatenate([h, m, h, l, h, m, extra, zero], 0)


def left_rows(x):
    term = -KAPPA * jnp.sum(x * x, 0, keepdims=True)
    return stack((2.0 * KAPPA) * x, term, True).astype(f32).T.astype(bf16)


def spread(row):
    return jnp.broadcast_to(row, (128, 128)).T


def block(j, width=128):
    return slice(j * width, (j + 1) * width)


def place(index):
    return {"row": index // 32, "col": lax.rem(index, 32)}


def remote(src, dst, ssem, rsem, where):
    return pltpu.make_async_remote_copy(src_ref=src, dst_ref=dst, send_sem=ssem, recv_sem=rsem, device_id=where,
                                        device_id_type=MESH)


def each(n, body):
    def step(i, c):
        body(i)
        return c

    lax.fori_loop(0, n, step, 0)


def coarse_kernel(src_in, smass_in, tgt_in, tmass_in, req_ref, pts_ref, clu_ref,
                  ftab_ref, gtab_ref, tiles_ref, inc_ref,
                  src_all, smass_all, tgt_all, tmass_all, inc_s, blocks, out_buf,
                  a_scr, d0, d1, t0, t1, ys, xs, gp, lb, acc, fst, am, mxs, fls, rs, sbuf, rbuf, fs_buf, fr_buf,
                  send_sem, recv_sem, fsend, frecv, cs_sem, cr_sem, qs_sem, qr_sem, bs_sem, br_sem, lsem):
    row = lax.axis_index("row")
    col = lax.axis_index("col")
    me = row * 32 + col
    core = lax.rem(col, 2)
    partner = {"row": row, "col": col + 1 - 2 * core}
    barrier = pltpu.get_barrier_semaphore()
    each(DEV - 1, lambda d: pl.semaphore_signal(barrier, inc=1, device_id=place(lax.rem(me + d + 1, DEV)),
                                                device_id_type=MESH))
    half = pl.ds(pl.multiple_of(core * 512, 512), 512)

    def tgt_copy(d, a):
        where = {"row": row, "col": lax.rem(col + d + 1, 32)}
        src, dst = ((tgt_in, tgt_all), (tmass_in, tmass_all))[a]
        return remote(src, dst.at[col], cs_sem.at[d, a], cr_sem.at[d, a], where)

    def src_copy(d, a):
        where = {"row": lax.rem(row + d + 1, 4), "col": col}
        src, dst = ((src_in, src_all), (smass_in, smass_all))[a]
        return remote(src.at[:, half], dst.at[row], cs_sem.at[31 + d, a], cr_sem.at[31 + d, a], where)

    def req_copy(d):
        to = lax.rem(me + d + 1, DEV)
        return remote(req_ref.at[to], inc_ref.at[me], qs_sem.at[d], qr_sem.at[d], place(to))

    def blk_copy(d):
        to = lax.rem(me + d + 1, DEV)
        return remote(out_buf.at[to], tiles_ref.at[me], bs_sem.at[d], br_sem.at[d], place(to))

    local = [pltpu.make_async_copy(tgt_in, tgt_all.at[col], lsem.at[0]),
             pltpu.make_async_copy(tmass_in, tmass_all.at[col], lsem.at[1]),
             pltpu.make_async_copy(src_in.at[:, half], src_all.at[row], lsem.at[2]),
             pltpu.make_async_copy(smass_in.at[:, half], smass_all.at[row], lsem.at[3]),
             pltpu.make_async_copy(req_ref.at[me], inc_ref.at[me], lsem.at[4])]
    for c in local:
        c.start()
    pl.semaphore_wait(barrier, DEV - 1)

    def start_src(d):
        src_copy(d, 0).start()
        src_copy(d, 1).start()

    def start_tgt(d):
        tgt_copy(d, 0).start()
        tgt_copy(d, 1).start()

    def wait_src(d):
        src_copy(d, 0).wait()
        src_copy(d, 1).wait()

    def wait_tgt(d):
        tgt_copy(d, 0).wait()
        tgt_copy(d, 1).wait()

    each(3, start_src)
    each(31, start_tgt)
    each(DEV - 1, lambda d: req_copy(d).start())
    for c in local:
        c.wait()
    each(3, wait_src)
    each(31, wait_tgt)
    for k in range(32):
        y = tgt_all[k]
        lbk = jnp.log2(tmass_all[k])
        ys[:, block(k)] = stack(y, lbk - KAPPA * jnp.sum(y * y, 0, keepdims=True), False)
        lb[:, block(k)] = jnp.broadcast_to(lbk, (8, 128))
    for q in range(4):
        for h in range(4):
            r0 = q * 512 + h * 128
            xs[r0:r0 + 128, :] = left_rows(src_all[q, :, block(h)])
            am[r0:r0 + 128, :] = spread(smass_all[q, :, block(h)])

    for t in range(TB_DEV):
        for h in range(2):
            blocks[t, h * 16:h * 16 + 16, :] = pts_ref[:, block(2 * t + h)]
    each(DEV - 1, lambda d: req_copy(d).wait())
    to_scalar = pltpu.make_async_copy(inc_ref, inc_s, lsem.at[5])
    to_scalar.start()
    to_scalar.wait()

    def fill(p):
        for q in range(2):
            t = inc_s[p, 0, 4 + q]
            out_buf[p, q * 32:q * 32 + 32, :] = blocks[t]
            out_buf[p, 64 + 2 * q:66 + 2 * q, :] = clu_ref[t].astype(f32)
        out_buf[p, 68:72, :] = jnp.zeros((4, 128), f32)

    each(DEV, fill)
    each(DEV - 1, lambda d: blk_copy(d).start())
    own = pltpu.make_async_copy(out_buf.at[me], tiles_ref.at[me], lsem.at[6])
    own.start()

    acc[...] = jnp.full_like(acc, -jnp.inf)
    d1[192:, :] = jnp.zeros((CH, KT), f32)
    fls[...] = jnp.full_like(fls, -jnp.inf)

    def product(dst, b, quarter):
        xc = xs[pl.ds(pl.multiple_of(b * 256, 256), 256), :]
        for u in range(4):
            c0 = quarter * 1024 + u * 256
            dst[:, c0:c0 + 256] = jnp.dot(xc, ys[:, c0:c0 + 256], preferred_element_type=f32)

    def rows_of(n):
        return pl.ds(pl.multiple_of(n * CH, CH), CH)

    def top(src, q):
        rr = block(q, CH)
        mx = src[rr, block(0)]
        for j in range(1, NJ):
            mx = jnp.maximum(mx, src[rr, block(j)])
        mxs[...] = jnp.broadcast_to(jnp.max(mx, 1, keepdims=True), (CH, 128))

    def keep(src, q, rows, fl, j):
        v = src[block(q, CH), block(j)] + fl
        a_scr[rows, block(j)] = v
        acc[:, block(j)] = jnp.maximum(acc[:, block(j)], jnp.max(v.reshape(CH // 8, 8, 128), 0))

    def step(n, q, now, before, b_next, nxt, after, q_after):
        prev = rows_of(lax.rem(n + 31, 32))
        mx = mxs[...]
        fl = fls[...]
        s = None
        for j in range(NJ):
            e = jnp.exp2(now[block(q, CH), block(j)] - mx)
            s = e if s is None else s + e
            keep(before, (q + 3) % 4, prev, fl, j)
        product(nxt, b_next, q)
        s = jnp.broadcast_to(jnp.sum(s, 1, keepdims=True), (CH, 128))
        f1 = -(mx + jnp.log2(s))
        fst[rows_of(n), :] = f1
        fls[...] = f1 + jnp.log2(am[rows_of(n), :])
        top(after, q_after)

    for q in range(4):
        product(d0, 0, q)
    top(d0, 0)

    def pair(p):
        for q in range(4):
            step(8 * p + q, q, d0, d1 if q == 0 else d0, 2 * p + 1, d1, d1 if q == 3 else d0, (q + 1) % 4)
        for q in range(4):
            step(8 * p + 4 + q, q, d1, d0 if q == 0 else d1, lax.rem(2 * p + 2, 8), d0, d0 if q == 3 else d1,
                 (q + 1) % 4)

    each(4, pair)
    fl = fls[...]
    for j in range(NJ):
        keep(d1, 3, rows_of(31), fl, j)
    for j in range(NJ):
        gp[:, block(j)] = jnp.broadcast_to(jnp.max(acc[:, block(j)], 0, keepdims=True), (8, 128))
    acc[...] = jnp.zeros_like(acc)

    def second(c):
        for j in range(NJ):
            v = a_scr[rows_of(c), block(j)].reshape(CH // 8, 8, 128) - gp[:, block(j)][None]
            acc[:, block(j)] = acc[:, block(j)] + jnp.sum(jnp.exp2(v), 0)

    each(HALF // CH, second)
    for j in range(NJ):
        sbuf[0, :, block(j)] = gp[:1, block(j)] + jnp.log2(jnp.sum(acc[:, block(j)], 0, keepdims=True))

    def swap(k):
        cp = remote(sbuf.at[k], rbuf.at[k], send_sem.at[k], recv_sem.at[k], partner)
        cp.start()
        cp.wait()

    swap(0)
    for j in range(NJ):
        l0, l1 = sbuf[0, :, block(j)], rbuf[0, :, block(j)]
        m = jnp.maximum(l0, l1)
        l = m + jnp.log2(jnp.exp2(l0 - m) + jnp.exp2(l1 - m))
        gp[:, block(j)] = lb[:, block(j)] - jnp.broadcast_to(l, (8, 128))

    def turn(k, restab, last):
        acc[...] = jnp.zeros_like(acc)

        def score(t, rows, j):
            v = a_scr[rows, block(j)].reshape(CH // 8, 8, 128) + gp[:, block(j)][None]
            e = jnp.exp2(v).reshape(CH, 128)
            t[:, block(j)] = e
            return e

        def both(tn, rn, tp, rp):
            r = rs[...]
            u = am[rp, :] / jnp.broadcast_to(jnp.sum(r, 1, keepdims=True), (CH, 128))
            if restab or last:
                shift = -jnp.log2(u)
                fst[rp, :] = fst[rp, :] - shift
            r = None
            for j in range(NJ):
                e = score(tn, rn, j)
                r = e if r is None else r + e
                acc[:, block(j)] = acc[:, block(j)] + jnp.sum((tp[:, block(j)] * u).reshape(CH // 8, 8, 128), 0)
                if restab:
                    a_scr[rp, block(j)] = a_scr[rp, block(j)] - shift
            rs[...] = r

        r = score(t0, rows_of(0), 0)
        for j in range(1, NJ):
            r = r + score(t0, rows_of(0), j)
        rs[...] = r

        def chunk(c):
            both(t1, rows_of(2 * c + 1), t0, rows_of(2 * c))
            both(t0, rows_of(lax.rem(2 * c + 2, 32)), t1, rows_of(2 * c + 1))

        each(HALF // CH // 2, chunk)
        for j in range(NJ):
            sbuf[k, :, block(j)] = jnp.sum(acc[:, block(j)], 0, keepdims=True)
        swap(k)
        for j in range(NJ):
            c = jnp.broadcast_to(sbuf[k, :, block(j)] + rbuf[k, :, block(j)], (8, 128))
            gp[:, block(j)] = gp[:, block(j)] + (lb[:, block(j)] - jnp.log2(c))

    each(2, lambda i: turn(i + 1, False, False))
    turn(3, True, False)
    each(3, lambda i: turn(i + 4, False, False))
    turn(7, False, True)
    for h in range(16):
        fs_buf[h:h + 1, :] = (fst[block(h), :] * UNIT).T[:1, :]
    cp = remote(fs_buf, fr_buf, fsend, frecv, partner)
    cp.start()
    for j in range(NJ):
        gtab_ref[j:j + 1, :] = gp[:1, block(j)] * UNIT
    cp.wait()
    for q in range(4):
        a, b = fs_buf[q * 4:q * 4 + 4], fr_buf[q * 4:q * 4 + 4]
        ftab_ref[q * 8:q * 8 + 4, :] = jnp.where(core == 0, a, b)
        ftab_ref[q * 8 + 4:q * 8 + 8, :] = jnp.where(core == 0, b, a)
    own.wait()
    each(DEV - 1, lambda d: blk_copy(d).wait())


def coarse(src_cent, src_mass, tgt_cent, tgt_mass, req, tgt_pts, tgt_cluster):
    V = pltpu.VMEM
    S = jax.ShapeDtypeStruct
    dma = pltpu.SemaphoreType.DMA
    return pl.pallas_call(
        coarse_kernel,
        out_shape=(S((32, 128), f32), S((32, 128), f32), S((DEV, 72, 128), f32), S((DEV, 1, 128), i32)),
        in_specs=[VMEM] * 7,
        out_specs=(VMEM, VMEM, pl.BlockSpec(memory_space=pl.ANY), VMEM),
        scratch_shapes=[V((4, F, 512), f32), V((4, 1, 512), f32), V((32, F, 128), f32), V((32, 1, 128), f32),
                        pltpu.SMEM((DEV, 1, 128), i32), V((TB_DEV, 32, 128), f32), V((DEV, 72, 128), f32),
                        V((HALF, KT), f32), V((256, KT), f32), V((256, KT), f32), V((CH, KT), f32), V((CH, KT), f32),
                        V((128, KT), bf16), V((HALF, 128), bf16), V((8, KT), f32), V((8, KT), f32), V((8, KT), f32),
                        V((HALF, 128), f32), V((HALF, 128), f32), V((CH, 128), f32), V((CH, 128), f32),
                        V((CH, 128), f32), V((8, 1, KT), f32), V((8, 1, KT), f32),
                        V((16, 128), f32), V((16, 128), f32), dma((8,)), dma((8,)), dma, dma,
                        dma((34, 2)), dma((34, 2)), dma((DEV,)), dma((DEV,)), dma((DEV,)), dma((DEV,)), dma((7,))],
        compiler_params=pltpu.CompilerParams(collective_id=1, has_side_effects=True,
                                             vmem_limit_bytes=62 * 1024 * 1024),
        name="coarse",
    )(src_cent, src_mass.reshape(1, -1), tgt_cent, tgt_mass.reshape(1, -1), req, tgt_pts,
      tgt_cluster.reshape(TB_DEV, 2, 128))


def request_kernel(sup_ref, req_ref, slot_ref):
    wanted = sup_ref[...].astype(f32)
    owner = jnp.floor(wanted * (1.0 / TB_DEV))
    local = wanted - owner * TB_DEV
    sub = lax.broadcasted_iota(i32, (128, 128), 0)
    lane = lax.broadcasted_iota(i32, (128, 128), 1)
    lanef = lane.astype(f32)
    same = jnp.broadcast_to(owner, (128, 128)) == sub.astype(f32)
    lo = jnp.min(jnp.where(same, lanef, 1e6), 1, keepdims=True)
    hi = jnp.max(jnp.where(same, lanef, -1.0), 1, keepdims=True)
    locb = jnp.broadcast_to(local, (128, 128)) + 1.0
    id0 = jnp.sum(jnp.where(lanef == lo, locb, 0.0), 1, keepdims=True) - 1.0
    id1 = jnp.sum(jnp.where((lanef == hi) & (hi > lo), locb, 0.0), 1, keepdims=True) - 1.0
    some = jnp.maximum(hi, 0.0)
    row = jnp.where(lane == 0, id0, jnp.where(lane == 1, id1, jnp.where(lane == 2, jnp.minimum(lo, some), jnp.where(
        lane == 3, some, jnp.where(lane == 4, jnp.maximum(id0, 0.0), jnp.maximum(id1, 0.0))))))
    req_ref[:, 0, :] = row.astype(i32)
    ownc = spread(owner)
    before = jnp.where((ownc == jnp.broadcast_to(owner, (128, 128))) & (sub < lane), 1.0, 0.0)
    second = jnp.sum(before, 0, keepdims=True)
    out = jnp.concatenate([owner * 9.0 + second * 4.0, second, owner * 9.0 + 8.0, owner], 0)
    slot_ref[...] = out.astype(i32)


def make_requests(support):
    return pl.pallas_call(
        request_kernel,
        out_shape=(jax.ShapeDtypeStruct((128, 1, 128), i32), jax.ShapeDtypeStruct((4, 128), i32)),
        in_specs=[VMEM], out_specs=(VMEM, VMEM), name="make_requests",
    )(support.reshape(1, 128))


def lookup(tab, idx):
    low = idx & 127
    high = idx >> 7
    out = jnp.zeros((8, 128), f32)
    for r in range(32):
        got = jnp.take_along_axis(jnp.broadcast_to(tab[r:r + 1, :], (8, 128)), low, axis=1)
        out = jnp.where(high == r, got, out)
    return out


def fine_kernel(slot_ref, req_ref, ftab_ref, gtab_ref, src_ref, sclu_ref, tile_ref, oclu_ref, inc_ref,
                cf_ref, cg_ref, ff_ref, fg_ref,
                gs, fs, sg, ccl, xt0, xt1, fx0, fx1, sc0, sc1, rm0, rm1, sa, lse, back, ret, idr, mt, ex,
                ssem, rsem, lsem):
    row = lax.axis_index("row")
    col = lax.axis_index("col")
    me = row * 32 + col
    barrier = pltpu.get_barrier_semaphore()
    each(DEV - 1, lambda d: pl.semaphore_signal(barrier, inc=1, device_id=place(lax.rem(me + d + 1, DEV)),
                                                device_id_type=MESH))
    cf_ref[...] = ftab_ref[pl.ds(pl.multiple_of(row * 8, 8), 8), :]
    cg_ref[...] = gtab_ref[pl.ds(col, 1), :]
    ft = ftab_ref[...] * KAPPA
    gt = gtab_ref[...] * KAPPA

    def clusters(e):
        both = tile_ref[slot_ref[2, e]]
        second = slot_ref[1, e].astype(f32) > 0.5
        ccl[e] = jnp.where(second, both[2:4], both[0:2])

    each(DEV, clusters)
    for r in range(2):
        fs[block(r, 8), :] = lookup(ft, sclu_ref[block(r, 8), :])

    def own(r):
        rows = pl.ds(pl.multiple_of(r * 8, 8), 8)
        sg[rows, :] = lookup(gt, oclu_ref[rows, :])

    each(8, own)

    def sent(r):
        rows = pl.ds(pl.multiple_of(r * 4, 4), 4)
        gs[rows, :, :] = lookup(gt, ccl[rows, :, :].reshape(8, 128).astype(i32)).reshape(4, 2, 128)

    each(32, sent)

    def left(b, xt, fx):
        for h in range(2):
            xt[block(h), :] = left_rows(src_ref[:, pl.ds(pl.multiple_of(b * BLK + h * 128, 128), 128)])
            fx[block(h), :] = spread(fs[pl.ds(2 * b + h, 1), :])

    def duals(e):
        return [gs[e, h:h + 1, :] for h in range(2)]

    def product(b, k, xt, sc, rm):
        e = b * SUPP + k
        i = slot_ref[0, e]
        part = [jnp.concatenate([tile_ref[i + 2 * h], tile_ref[i + 2 * h + 1]], 0) for h in range(2)]
        y = jnp.concatenate(part, 1)
        st = stack(y, jnp.concatenate(duals(e), 1) - KAPPA * jnp.sum(y * y, 0, keepdims=True), False)
        d = jnp.dot(xt[...], st, preferred_element_type=f32)
        sc[k] = d
        rm[...] = jnp.maximum(rm[...], jnp.maximum(d[:, :128], d[:, 128:]))

    def col_part(b, k, sc, fx):
        g = duals(b * SUPP + k)
        for h in range(2):
            v = sc[k, :, block(h)] + fx[...]
            m = jnp.max(v, 0, keepdims=True)
            s = jnp.sum(jnp.exp2(v - m), 0, keepdims=True)
            lse[b * SUPP + k, h:h + 1, :] = m + jnp.log2(s) - g[h]

    def row_part(k, sc, rm):
        m = rm[...]
        return jnp.exp2(sc[k, :, :128] - m) + jnp.exp2(sc[k, :, 128:] - m)

    def one(b, xt, fx, sc, rm, prev):
        left(b, xt, fx)
        rm[...] = jnp.full_like(rm, -jnp.inf)
        product(b, 0, xt, sc, rm)
        product(b, 1, xt, sc, rm)
        if prev is not None:
            sa[...] = jnp.zeros_like(sa)

        def some(g):
            if prev is not None:
                sa[...] = sa[...] + row_part(2 * g, *prev) + row_part(2 * g + 1, *prev)
            for u in range(2):
                col_part(b, 2 * g + u, sc, fx)
            for u in range(2):
                product(b, lax.rem(2 * g + 2 + u, SUPP), xt, sc, rm)

        each(SUPP // 2, some)
        rm[...] = jnp.broadcast_to(jnp.max(rm[...], 1, keepdims=True), (BLK, 128))
        if prev is not None:
            finish(b - 1, prev[1])

    def finish(b, rm):
        out = rm[...] + jnp.log2(jnp.sum(sa[...], 1, keepdims=True)) - math.log2(SUPP * BLK)
        for h in range(2):
            ff_ref[pl.ds(2 * b + h, 1), :] = (0.5 * UNIT) * (fs[pl.ds(2 * b + h, 1), :] - out[block(h), :].T[:1, :])

    one(0, xt0, fx0, sc0, rm0, None)

    def two(p):
        one(2 * p + 1, xt1, fx1, sc1, rm1, (sc0, rm0))
        one(2 * p + 2, xt0, fx0, sc0, rm0, (sc1, rm1))

    each(3, two)
    one(7, xt1, fx1, sc1, rm1, (sc0, rm0))

    def fill(p):
        for q in range(2):
            back[p, 2 * q:2 * q + 2, :] = lse[req_ref[p, 0, 2 + q]]

    each(DEV, fill)

    def ret_copy(d):
        to = lax.rem(me + d + 1, DEV)
        return remote(back.at[to], ret.at[me], ssem.at[d], rsem.at[d], place(to))

    pl.semaphore_wait(barrier, DEV - 1)
    each(DEV - 1, lambda d: ret_copy(d).start())
    mine = pltpu.make_async_copy(back.at[me], ret.at[me], lsem)
    mine.start()
    sa[...] = jnp.zeros_like(sa)

    def last(k):
        sa[...] = sa[...] + row_part(k, sc1, rm1)

    each(SUPP, last)
    finish(7, rm1)
    lane = lax.broadcasted_iota(i32, (DEV, 128), 1).astype(f32)
    sub = lax.broadcasted_iota(i32, (DEV, 128), 0).astype(f32)
    hot, hot_t = [], []
    for q in range(2):
        idv = jnp.broadcast_to(inc_ref[:, 0, q:q + 1].astype(f32), (DEV, 128))
        idr[q] = idv
        hot.append(jnp.where(idv == lane, 1.0, 0.0).astype(bf16))
        hot_t.append(jnp.where(idv.T == sub, 1.0, 0.0).astype(bf16))
    count = sum(jnp.sum(h.astype(f32), 1, keepdims=True) for h in hot_t)
    mt[...] = jnp.zeros_like(mt)
    mine.wait()
    each(DEV - 1, lambda d: ret_copy(d).wait())
    for q in range(2):
        for h in range(2):
            ex[q, h] = ret[:, 2 * q + h, :]

    def tops(t):
        tf = t.astype(f32)
        for h in range(2):
            m = jnp.maximum(jnp.where(idr[0] == tf, ex[0, h], -jnp.inf), jnp.where(idr[1] == tf, ex[1, h], -jnp.inf))
            mt[h, pl.ds(t, 1), :] = jnp.max(m, 0, keepdims=True)

    each(TB_DEV, tops)
    for h in range(2):
        tot = jnp.zeros((DEV, 128), f32)
        mparts = split3(mt[h])
        for q in range(2):
            mx = sum(jnp.dot(hot[q], mp, preferred_element_type=f32) for mp in mparts)
            e = jnp.where(idr[q] >= 0.0, jnp.exp2(ex[q, h] - mx), 0.0)
            tot = tot + sum(jnp.dot(hot_t[q], ep, preferred_element_type=f32) for ep in split3(e))
        ex[0, h] = mt[h] + jnp.log2(tot) - jnp.log2(jnp.broadcast_to(count, (DEV, 128)) * BLK)
    for t in range(TB_DEV):
        for h in range(2):
            fg_ref[2 * t + h:2 * t + h + 1, :] = (0.5 * UNIT) * (sg[2 * t + h:2 * t + h + 1, :] - ex[0, h, t:t + 1, :])


def fine(slots, req, ftab, gtab, src_pts, src_cluster, tiles, tgt_cluster, incoming):
    S = jax.ShapeDtypeStruct
    V = pltpu.VMEM
    dma = pltpu.SemaphoreType.DMA
    return pl.pallas_call(
        fine_kernel,
        out_shape=(S((8, 128), f32), S((1, 128), f32), S((16, 128), f32), S((64, 128), f32)),
        in_specs=[SMEM, SMEM] + [VMEM] * 7,
        out_specs=(VMEM,) * 4,
        scratch_shapes=[V((DEV, 2, 128), f32), V((16, 128), f32), V((64, 128), f32), V((DEV, 2, 128), f32),
                        V((BLK, 128), bf16), V((BLK, 128), bf16), V((BLK, 128), f32), V((BLK, 128), f32),
                        V((SUPP, BLK, BLK), f32), V((SUPP, BLK, BLK), f32), V((BLK, 128), f32), V((BLK, 128), f32),
                        V((BLK, 128), f32), V((DEV, 2, 128), f32), V((DEV, 4, 128), f32), V((DEV, 4, 128), f32),
                        V((2, DEV, 128), f32), V((2, DEV, 128), f32), V((2, 2, DEV, 128), f32),
                        dma((DEV,)), dma((DEV,)), dma],
        compiler_params=pltpu.CompilerParams(collective_id=2, has_side_effects=True,
                                             vmem_limit_bytes=48 * 1024 * 1024),
        name="fine",
    )(slots, req, ftab, gtab, src_pts, src_cluster.reshape(16, 128), tiles.reshape(DEV * 9, 8, 128), tgt_cluster.reshape(64, 128), incoming)


def on_device(src_cent, tgt_cent, src_mass, tgt_mass, src_pts, tgt_pts, src_cluster, tgt_cluster, support):
    req, slots = make_requests(support)
    ftab, gtab, tiles, incoming = coarse(src_cent, src_mass, tgt_cent, tgt_mass, req, tgt_pts, tgt_cluster)
    cf, cg, ff, fg = fine(slots, req, ftab, gtab, src_pts, src_cluster, tiles, tgt_cluster, incoming)
    return cf.reshape(-1), cg.reshape(-1), ff.reshape(-1), fg.reshape(-1)


def solution(mesh):
    both = ("row", "col")
    in_specs = (P(None, "row"), P(None, "col"), P("row"), P("col"), P(None, both), P(None, both), P(both), P(both),
                P(both, None))
    out_specs = (P("row"), P("col"), P(both), P(both))
    return jax.shard_map(on_device, mesh=mesh, in_specs=in_specs, out_specs=out_specs, check_vma=False)
```

time: 213 us -> 193 us (0.906)
  blocking collectives: 41.2 us -> 0 us
  Pallas kernels: 156 us -> 180 us
  starting transfers between devices: 12.7 us -> 0 us
  local copies, waits for them, and re-layouts: 2.01 us -> 12.1 us
    all_to_all x2 -> x0, blocking collectives: 41.2 us -> none  [exchange(): lax.all_to_all(x, ('row', 'col'), split_axis=0, concat_axis=0, tiled=True)]
    pallas_call x5 -> x2, Pallas kernels: 113 us -> 126 us  [the longest x1 125 us: coarse(): pl.pallas_call(coarse_kernel, out_shape=(S((32, 128), f32), S((32, 128),...]
    all_to_all x2 -> x0, starting transfers between devices: 12.7 us -> none  [exchange(): lax.all_to_all(x, ('row', 'col'), split_axis=0, concat_axis=0, tiled=True)]
    pallas_call x1, Pallas kernels: 43 us -> 54.1 us  [fine(): pl.pallas_call(fine_kernel, out_shape=(S((8, 128), f32), S((1, 128), f32)...]
    unnamed x2 -> x22, local copies, waits for them, and re-layouts: 0.73 us -> 10.8 us
  transfers between devices with their start and end apart: 2 -> 0, of which waited for: 0 -> 0; matrix products, arithmetic and copies ran while one was open for 0% -> 0% of each run, Pallas kernels for 47% -> 0%
where the time goes in v2:
time: 193 us
  Pallas kernels  180 us (93%)
  local copies, waits for them, and re-layouts  12.1 us (6%)
    pallas_call x1, Pallas kernels, coarse(): pl.pallas_call(coarse_kernel, out_shape=(S((32, 128), f32), S((32, 128),...  125 us
    pallas_call x1, Pallas kernels, fine(): pl.pallas_call(fine_kernel, out_shape=(S((8, 128), f32), S((1, 128), f32)...  54.1 us
    unnamed x22, local copies, waits for them, and re-layouts  10.8 us

profile of v2, /device:TPU:1, one launch (start us, length us, event | category | flops | bytes accessed | tf_op | source)
XLA Modules:
  0.0 192.9 jit_solution(13109760377314829150)
XLA Ops:
  0.6 1.3 reshape.41.sup_ref
  1.9 1.5 make_requests.1
  3.4 124.5 %coarse.1 = (f32[32,128]{1,0:T(8,128)}, f32[32,128]{1,0:T(8,128)}, f32[128,72,128]{2,1,0:T(8,128)}, s32[128,1,128]{2,1,0:T(1,128)}) custom-call(f32[16,1024]{1,0:T(8,128)} %src_in.1, f32[1,1024]{1,0:T(1,128)} %bitcast.18, f32[16,128]{1,0:T(8,128)} %tgt_in.1, f32[1,128]{1,0:T(1,128)} %bitcast.19, s32[128,1,128]{2,1,0:T(1,128)} %get-tuple-element.15.req_ref, ...), custom_call_target="tpu_custom_call" | custom-call | tf_op jit(solution)/shard_map/coarse/pallas_call | solution.py:324
  127.9 0.0 copy-start
  127.9 2.3 %copy-done = f32[128,72,128]{2,1,0:T(8,128)S(1)} copy-done((f32[128,72,128]{2,1,0:T(8,128)S(1)}, f32[128,72,128]{2,1,0:T(8,128)}, u32[]{:S(2)}) %copy-start) | copy-done | bytes 4718616
  130.3 0.0 copy-start.1
  130.3 0.8 copy-done.1
  131.1 0.0 copy-start.2
  131.1 0.8 copy-done.2
  131.9 0.0 copy-start.3
  131.9 0.9 copy-done.3
  132.8 0.0 copy-start.4
  132.8 0.8 copy-done.4
  133.6 0.0 copy-start.5
  133.6 0.7 copy-done.5
  134.3 0.0 copy-start.6
  134.3 0.7 copy-done.6
  135.1 0.7 copy-done.7
  135.8 0.7 copy-done.8
  136.4 54.1 %fine.1 = (f32[8,128]{1,0:T(8,128)S(1)}, f32[1,128]{1,0:T(1,128)S(1)}, f32[16,128]{1,0:T(8,128)S(1)}, f32[64,128]{1,0:T(8,128)S(1)}) custom-call(s32[4,128]{1,0:T(4,128)S(1)} %copy-done.8, s32[128,1,128]{2,1,0:T(1,128)S(1)} %copy-done.1, f32[32,128]{1,0:T(8,128)S(1)} %copy-done.5, f32[32,128]{1,0:T(8,128)S(1)} %copy-done.6, f32[16,2048]{1,0:T(8,128)S(1)} %copy-done.3, ...), custom_call_target="tpu_custom_call" | custom-call | tf_op jit(solution)/shard_map/fine/pallas_call | solution.py:548
  190.5 0.6 copy.17
  191.1 0.5 copy.18
  191.7 0.6 copy.19
  192.3 0.6 copy.20
  (2 shorter events, 0.0 us)
Async XLA Ops:
  127.9 2.3 %copy-start = (f32[128,72,128]{2,1,0:T(8,128)S(1)}, f32[128,72,128]{2,1,0:T(8,128)}, u32[]{:S(2)}) copy-start(f32[128,72,128]{2,1,0:T(8,128)} %get-tuple-element.18) | copy-start | bytes 14155780
  130.3 0.8 copy-start.1
  131.1 0.8 copy-start.2
  131.9 0.9 copy-start.3
  132.8 0.8 copy-start.4
  133.6 0.7 copy-start.5
  134.3 0.7 copy-start.6
  135.1 0.7 copy-start.7
  135.7 0.7 copy-start.8

commit v3 on v2

v3 whole, which is shorter than its diff:
```python
import math

import jax
import jax.numpy as jnp
from jax import lax
from jax.experimental import pallas as pl
from jax.experimental.pallas import tpu as pltpu
from jax.sharding import PartitionSpec as P

MESH = pl.DeviceIdType.MESH
F = 16
BLK = 256
SUPP = 16
SB_DEV = 8
TB_DEV = 32
KS = 4096
KT = 4096
EPS = 0.1
KAPPA = math.log2(math.e) / EPS
UNIT = EPS * math.log(2.0)
DEV = 128
STRIDE = 37
UNR = 4
PART = KS // 4
CH = 64
NJ = KT // 128
VMEM = pl.BlockSpec(memory_space=pltpu.VMEM)
SMEM = pl.BlockSpec(memory_space=pltpu.SMEM)
f32 = jnp.float32
i32 = jnp.int32
bf16 = jnp.bfloat16


def split3(v):
    hi = v.astype(bf16)
    rest = v - hi.astype(f32)
    mid = rest.astype(bf16)
    return hi, mid, (rest - mid.astype(f32)).astype(bf16)


def stack(pts, term, left):
    h, m, l = split3(pts)
    n = pts.shape[1]
    th, tm, tl = [v.astype(f32) for v in split3(term)]
    rid = lax.broadcasted_iota(i32, (16, n), 0)
    base, ones = (0, 3) if left else (3, 0)
    extra = jnp.where(rid == base, th, jnp.where(rid == base + 1, tm, jnp.where(rid == base + 2, tl, 0.0)))
    extra = jnp.where((rid >= ones) & (rid < ones + 3), 1.0, extra).astype(bf16)
    zero = jnp.zeros((16, n), bf16)
    if left:
        return jnp.concatenate([h, h, m, h, l, m, extra, zero], 0)
    return jnp.concatenate([h, m, h, l, h, m, extra, zero], 0)


def left_rows(x, dual=0.0):
    term = dual - KAPPA * jnp.sum(x * x, 0, keepdims=True)
    return stack((2.0 * KAPPA) * x, term, True).astype(f32).T.astype(bf16)


def spread(row):
    return jnp.broadcast_to(row, (128, 128)).T


def block(j, width=128):
    return slice(j * width, (j + 1) * width)


def place(index):
    return {"row": lax.div(index, 32), "col": lax.rem(index, 32)}


def remote(src, dst, ssem, rsem, where):
    return pltpu.make_async_remote_copy(src_ref=src, dst_ref=dst, send_sem=ssem, recv_sem=rsem, device_id=where,
                                        device_id_type=MESH)


def each(n, body):
    def step(i, c):
        body(i)
        return c

    lax.fori_loop(0, n, step, 0)


def coarse_kernel(src_in, smass_in, tgt_in, tmass_in, req_ref, pts_ref, clu_ref,
                  ftab_ref, gtab_ref, tiles_ref, inc_ref,
                  src_all, smass_all, tgt_all, tmass_all, inc_s, blocks, out_buf,
                  a_scr, t0, t1, ys, xs, gp, lb, acc, fst, am, sh, mxs, rs, rbuf, fbuf,
                  send_sem, recv_sem, cs_sem, cr_sem, qs_sem, qr_sem, bs_sem, br_sem, lsem):
    row = lax.axis_index("row")
    col = lax.axis_index("col")
    me = row * 32 + col
    core = lax.rem(col, 2)
    quarter = lax.rem(row, 2) * 2 + core
    barrier = pltpu.get_barrier_semaphore()
    each(DEV - 1, lambda d: pl.semaphore_signal(barrier, inc=1, device_id=place(lax.rem(me + d + 1, DEV)),
                                                device_id_type=MESH))

    def quarter_of(r):
        return pl.ds(pl.multiple_of((lax.rem(r, 2) * 2 + core) * 256, 256), 256)


    def tgt_copy(d, a):
        where = {"row": row, "col": lax.rem(col + d + 1, 32)}
        src, dst = ((tgt_in, tgt_all), (tmass_in, tmass_all))[a]
        return remote(src, dst.at[col], cs_sem.at[d, a], cr_sem.at[d, a], where)

    def src_copy(d, a):
        to = lax.rem(row + d + 1, 4)
        src, dst = ((src_in, src_all), (smass_in, smass_all))[a]
        return remote(src.at[:, quarter_of(to)], dst.at[row], cs_sem.at[31 + d, a], cr_sem.at[31 + d, a],
                      {"row": to, "col": col})

    def req_copy(d):
        to = lax.rem(me + d + 1, DEV)
        return remote(req_ref.at[to], inc_ref.at[me], qs_sem.at[d], qr_sem.at[d], place(to))

    def blk_copy(d):
        to = lax.rem(me + lax.rem((d + 1) * STRIDE, DEV), DEV)
        return remote(out_buf.at[to], tiles_ref.at[me], bs_sem.at[d], br_sem.at[d], place(to))

    local = [pltpu.make_async_copy(tgt_in, tgt_all.at[col], lsem.at[0]),
             pltpu.make_async_copy(tmass_in, tmass_all.at[col], lsem.at[1]),
             pltpu.make_async_copy(src_in.at[:, quarter_of(row)], src_all.at[row], lsem.at[2]),
             pltpu.make_async_copy(smass_in.at[:, quarter_of(row)], smass_all.at[row], lsem.at[3]),
             pltpu.make_async_copy(req_ref.at[me], inc_ref.at[me], lsem.at[4])]
    for c in local:
        c.start()
    pl.semaphore_wait(barrier, DEV - 1)

    def start_src(d):
        src_copy(d, 0).start()
        src_copy(d, 1).start()

    def start_tgt(d):
        tgt_copy(d, 0).start()
        tgt_copy(d, 1).start()

    def wait_src(d):
        src_copy(d, 0).wait()
        src_copy(d, 1).wait()

    def wait_tgt(d):
        tgt_copy(d, 0).wait()
        tgt_copy(d, 1).wait()

    each(3, start_src)
    each(31, start_tgt)
    each(DEV - 1, lambda d: req_copy(d).start())
    for c in local:
        c.wait()
    each(3, wait_src)
    each(31, wait_tgt)
    for k in range(32):
        y = tgt_all[k]
        lbk = jnp.log2(tmass_all[k])
        ys[:, block(k)] = stack(y, lbk - KAPPA * jnp.sum(y * y, 0, keepdims=True), False)
        lb[:, block(k)] = jnp.broadcast_to(lbk, (8, 128))
    for q in range(4):
        for h in range(2):
            r0 = q * 256 + h * 128
            xs[r0:r0 + 128, :] = left_rows(src_all[q, :, block(h)])
            am[r0:r0 + 128, :] = spread(smass_all[q, :, block(h)])

    for t in range(TB_DEV):
        for h in range(2):
            blocks[t, h * 16:h * 16 + 16, :] = pts_ref[:, block(2 * t + h)]
    each(DEV - 1, lambda d: req_copy(d).wait())
    to_scalar = pltpu.make_async_copy(inc_ref, inc_s, lsem.at[5])
    to_scalar.start()
    to_scalar.wait()

    def fill(p):
        for q in range(2):
            t = inc_s[p, 0, 4 + q]
            out_buf[p, q * 32:q * 32 + 32, :] = blocks[t]
            out_buf[p, 64 + 2 * q:66 + 2 * q, :] = clu_ref[t].astype(f32)
        out_buf[p, 68:72, :] = jnp.zeros((4, 128), f32)

    each(DEV, fill)
    each(43, lambda d: blk_copy(d).start())
    own = pltpu.make_async_copy(out_buf.at[me], tiles_ref.at[me], lsem.at[6])
    own.start()

    acc[...] = jnp.full_like(acc, -jnp.inf)

    def rows_of(n):
        return pl.ds(pl.multiple_of(n * CH, CH), CH)

    def first(b):
        wide = pl.ds(pl.multiple_of(b * 256, 256), 256)
        mx = jnp.full((256, 128), -jnp.inf, f32)
        for c in range(NJ // 2):
            d = jnp.dot(xs[wide, :], ys[:, block(c, 256)], preferred_element_type=f32)
            a_scr[wide, block(c, 256)] = d
            mx = jnp.maximum(mx, jnp.maximum(d[:, :128], d[:, 128:]))
        mxs[...] = jnp.broadcast_to(jnp.max(mx, 1, keepdims=True), (256, 128))
        fl = None
        for q in range(5):
            now, prev = rows_of(4 * b + q), rows_of(4 * b + q - 1)
            s = None
            for j in range(NJ):
                if q < 4:
                    e = jnp.exp2(a_scr[now, block(j)] - mxs[block(q, CH), :])
                    s = e if s is None else s + e
                if q > 0:
                    v = a_scr[prev, block(j)] + fl
                    acc[:, block(j)] = jnp.maximum(acc[:, block(j)], jnp.max(v.reshape(CH // 8, 8, 128), 0))
            if q < 4:
                f1 = -(mxs[block(q, CH), :] + jnp.log2(jnp.broadcast_to(jnp.sum(s, 1, keepdims=True), (CH, 128))))
                fst[now, :] = f1
                fl = f1 + jnp.log2(am[now, :])

    each(PART // 256, first)
    for j in range(NJ):
        gp[:, block(j)] = jnp.broadcast_to(jnp.max(acc[:, block(j)], 0, keepdims=True), (8, 128))
    acc[...] = jnp.zeros_like(acc)

    def second(c):
        fl = fst[rows_of(c), :] + jnp.log2(am[rows_of(c), :])
        for j in range(NJ):
            v = a_scr[rows_of(c), block(j)] + fl
            a_scr[rows_of(c), block(j)] = v
            v = jnp.exp2(v.reshape(CH // 8, 8, 128) - gp[:, block(j)][None])
            acc[:, block(j)] = acc[:, block(j)] + jnp.sum(v, 0)

    each(PART // CH, second)
    for j in range(NJ):
        rbuf[0, quarter, :, block(j)] = gp[:1, block(j)] + jnp.log2(jnp.sum(acc[:, block(j)], 0, keepdims=True))

    def to_group(buf, k):
        out = []
        for d in range(3):
            to = lax.rem(quarter + d + 1, 4)
            where = {"row": row - lax.rem(row, 2) + lax.div(to, 2), "col": col - core + lax.rem(to, 2)}
            out.append(remote(buf, buf, send_sem.at[k, d], recv_sem.at[k, d], where))
        return out

    def swap(k, send=True):
        copies = to_group(rbuf.at[k, quarter], k)
        for c in copies:
            c.start()
        if send:
            each(12, lambda d: blk_copy(43 + 12 * k + d).start())
        for c in copies:
            c.wait()

    swap(0)
    for j in range(NJ):
        ls = [rbuf[0, i, :, block(j)] for i in range(4)]
        m = jnp.maximum(jnp.maximum(ls[0], ls[1]), jnp.maximum(ls[2], ls[3]))
        l = m + jnp.log2(sum(jnp.exp2(v - m) for v in ls))
        gp[:, block(j)] = lb[:, block(j)] - jnp.broadcast_to(l, (8, 128))

    def turn(k, renew=False, send=True):
        acc[...] = jnp.zeros_like(acc)

        def both(tn, n, tp, p):
            if tp is not None:
                rows = rows_of(p)
                u = am[rows, :] / jnp.broadcast_to(jnp.sum(rs[...], 1, keepdims=True), (CH, 128))
                sh[rows, :] = -jnp.log2(u)
            if tn is not None:
                rows = rows_of(n)
                if renew:
                    move = sh[rows, :]
                    fst[rows, :] = fst[rows, :] - move
            r = None
            for j in range(NJ):
                if tn is not None:
                    v = a_scr[rows, block(j)]
                    if renew:
                        v = v - move
                        a_scr[rows, block(j)] = v
                    e = jnp.exp2(v.reshape(CH // 8, 8, 128) + gp[:, block(j)][None]).reshape(CH, 128)
                    tn[:, block(j)] = e
                    r = e if r is None else r + e
                if tp is not None:
                    v = (tp[:, block(j)] * u).reshape(CH // 8, 8, 128)
                    acc[:, block(j)] = acc[:, block(j)] + jnp.sum(v, 0)
            if tn is not None:
                rs[...] = r

        def chunk(c):
            both(t1, 2 * c + 1, t0, 2 * c)
            both(t0, 2 * c + 2, t1, 2 * c + 1)

        last = PART // CH - 1
        both(t0, 0, None, None)
        each(last // 2, chunk)
        both(t1, last, t0, last - 1)
        both(None, None, t1, last)
        for j in range(NJ):
            rbuf[k, quarter, :, block(j)] = jnp.sum(acc[:, block(j)], 0, keepdims=True)
        swap(k, send)
        for j in range(NJ):
            c = jnp.broadcast_to(sum(rbuf[k, i, :, block(j)] for i in range(4)), (8, 128))
            gp[:, block(j)] = gp[:, block(j)] + (lb[:, block(j)] - jnp.log2(c))

    each(3, lambda i: turn(i + 1))
    turn(4, renew=True)
    each(2, lambda i: turn(i + 5))
    turn(7, send=False)
    for h in range(8):
        fbuf[quarter, h:h + 1, :] = ((fst[block(h), :] - sh[block(h), :]) * UNIT).T[:1, :]
    copies = to_group(fbuf.at[quarter], 8)
    for c in copies:
        c.start()
    for j in range(NJ):
        gtab_ref[j:j + 1, :] = gp[:1, block(j)] * UNIT
    for c in copies:
        c.wait()
    for q in range(4):
        for i in range(4):
            ftab_ref[q * 8 + 2 * i:q * 8 + 2 * i + 2, :] = fbuf[i, 2 * q:2 * q + 2, :]
    own.wait()
    each(DEV - 1, lambda d: blk_copy(d).wait())


def coarse(src_cent, src_mass, tgt_cent, tgt_mass, req, tgt_pts, tgt_cluster):
    V = pltpu.VMEM
    S = jax.ShapeDtypeStruct
    dma = pltpu.SemaphoreType.DMA
    return pl.pallas_call(
        coarse_kernel,
        out_shape=(S((32, 128), f32), S((32, 128), f32), S((DEV, 72, 128), f32), S((DEV, 1, 128), i32)),
        in_specs=[VMEM] * 7,
        out_specs=(VMEM, VMEM, pl.BlockSpec(memory_space=pl.ANY), VMEM),
        scratch_shapes=[V((4, F, 256), f32), V((4, 1, 256), f32), V((32, F, 128), f32), V((32, 1, 128), f32),
                        pltpu.SMEM((DEV, 1, 128), i32), V((TB_DEV, 32, 128), f32), V((DEV, 72, 128), f32),
                        V((PART, KT), f32), V((CH, KT), f32), V((CH, KT), f32),
                        V((128, KT), bf16), V((PART, 128), bf16), V((8, KT), f32), V((8, KT), f32), V((8, KT), f32),
                        V((PART, 128), f32), V((PART, 128), f32), V((PART, 128), f32), V((256, 128), f32), V((CH, 128), f32),
                        V((8, 4, 1, KT), f32), V((4, 8, 128), f32),
                        dma((9, 3)), dma((9, 3)),
                        dma((34, 2)), dma((34, 2)), dma((DEV,)), dma((DEV,)), dma((DEV,)), dma((DEV,)), dma((7,))],
        compiler_params=pltpu.CompilerParams(collective_id=1, has_side_effects=True,
                                             vmem_limit_bytes=62 * 1024 * 1024),
        name="coarse",
    )(src_cent, src_mass.reshape(1, -1), tgt_cent, tgt_mass.reshape(1, -1), req, tgt_pts,
      tgt_cluster.reshape(TB_DEV, 2, 128))


def request_kernel(sup_ref, req_ref, slot_ref):
    wanted = sup_ref[...].astype(f32)
    owner = jnp.floor(wanted * (1.0 / TB_DEV))
    local = wanted - owner * TB_DEV
    sub = lax.broadcasted_iota(i32, (128, 128), 0)
    lane = lax.broadcasted_iota(i32, (128, 128), 1)
    lanef = lane.astype(f32)
    same = jnp.broadcast_to(owner, (128, 128)) == sub.astype(f32)
    lo = jnp.min(jnp.where(same, lanef, 1e6), 1, keepdims=True)
    hi = jnp.max(jnp.where(same, lanef, -1.0), 1, keepdims=True)
    locb = jnp.broadcast_to(local, (128, 128)) + 1.0
    id0 = jnp.sum(jnp.where(lanef == lo, locb, 0.0), 1, keepdims=True) - 1.0
    id1 = jnp.sum(jnp.where((lanef == hi) & (hi > lo), locb, 0.0), 1, keepdims=True) - 1.0
    some = jnp.maximum(hi, 0.0)
    row = jnp.where(lane == 0, id0, jnp.where(lane == 1, id1, jnp.where(lane == 2, jnp.minimum(lo, some), jnp.where(
        lane == 3, some, jnp.where(lane == 4, jnp.maximum(id0, 0.0), jnp.maximum(id1, 0.0))))))
    req_ref[:, 0, :] = row.astype(i32)
    ownc = spread(owner)
    before = jnp.where((ownc == jnp.broadcast_to(owner, (128, 128))) & (sub < lane), 1.0, 0.0)
    second = jnp.sum(before, 0, keepdims=True)
    out = jnp.concatenate([owner * 9.0 + second * 4.0, second, owner * 9.0 + 8.0, owner], 0)
    slot_ref[...] = out.astype(i32)


def make_requests(support):
    return pl.pallas_call(
        request_kernel,
        out_shape=(jax.ShapeDtypeStruct((128, 1, 128), i32), jax.ShapeDtypeStruct((4, 128), i32)),
        in_specs=[VMEM], out_specs=(VMEM, VMEM), name="make_requests",
    )(support.reshape(1, 128))


def lookup(tab, idx):
    low = idx & 127
    high = idx >> 7
    out = jnp.zeros((8, 128), f32)
    for r in range(32):
        got = jnp.take_along_axis(jnp.broadcast_to(tab[r:r + 1, :], (8, 128)), low, axis=1)
        out = jnp.where(high == r, got, out)
    return out


def fine_kernel(slot_ref, req_ref, ftab_ref, gtab_ref, src_ref, sclu_ref, tile_hbm, oclu_ref, inc_ref,
                cf_ref, cg_ref, ff_ref, fg_ref,
                tile_ref, gs, fs, sg, ccl, xt0, xt1, cm, sc0, sc1, rm0, rm1, sa, lse, back, ret, idr, mt, ex,
                ssem, rsem, lsem, tsem):
    fetch = pltpu.make_async_copy(tile_hbm, tile_ref, tsem)
    fetch.start()
    row = lax.axis_index("row")
    col = lax.axis_index("col")
    me = row * 32 + col
    barrier = pltpu.get_barrier_semaphore()
    each(DEV - 1, lambda d: pl.semaphore_signal(barrier, inc=1, device_id=place(lax.rem(me + d + 1, DEV)),
                                                device_id_type=MESH))
    cf_ref[...] = ftab_ref[pl.ds(pl.multiple_of(row * 8, 8), 8), :]
    cg_ref[...] = gtab_ref[pl.ds(col, 1), :]
    ft = ftab_ref[...] * KAPPA
    gt = gtab_ref[...] * KAPPA

    def clusters(e):
        both = tile_ref[slot_ref[2, e]]
        second = slot_ref[1, e].astype(f32) > 0.5
        ccl[pl.ds(2 * e, 2), :] = jnp.where(second, both[2:4], both[0:2])

    for r in range(2):
        fs[block(r, 8), :] = lookup(ft, sclu_ref[block(r, 8), :])

    def own(r):
        rows = pl.ds(pl.multiple_of(r * 8, 8), 8)
        sg[rows, :] = lookup(gt, oclu_ref[rows, :])

    each(8, own)
    fetch.wait()
    each(DEV, clusters)

    def sent(r):
        rows = pl.ds(pl.multiple_of(r * 8, 8), 8)
        gs[rows, :] = lookup(gt, ccl[rows, :].astype(i32))

    each(32, sent)

    def left(b, xt):
        for h in range(2):
            x = src_ref[:, pl.ds(pl.multiple_of(b * BLK + h * 128, 128), 128)]
            xt[block(h), :] = left_rows(x, fs[pl.ds(2 * b + h, 1), :])

    def duals(e):
        return [gs[pl.ds(2 * e + h, 1), :] for h in range(2)]

    def product(b, k, xt, sc, rm, cm):
        e = b * SUPP + k
        i = slot_ref[0, e]
        part = [jnp.concatenate([tile_ref[i + 2 * h], tile_ref[i + 2 * h + 1]], 0) for h in range(2)]
        y = jnp.concatenate(part, 1)
        st = stack(y, jnp.concatenate(duals(e), 1) - KAPPA * jnp.sum(y * y, 0, keepdims=True), False)
        d = jnp.dot(xt[...], st, preferred_element_type=f32)
        sc[k] = d
        rm[...] = jnp.maximum(rm[...], jnp.maximum(d[:, :128], d[:, 128:]))
        cm[k] = jnp.broadcast_to(jnp.max(d, 0, keepdims=True), (8, BLK))

    def col_part(b, k, sc, cm):
        g = duals(b * SUPP + k)
        for h in range(2):
            m = cm[k, :, block(h)]
            s = jnp.sum(jnp.exp2(sc[k, :, block(h)].reshape(BLK // 8, 8, 128) - m[None]), 0)
            lse[b * SUPP + k, h:h + 1, :] = m[:1] + jnp.log2(jnp.sum(s, 0, keepdims=True)) - g[h]

    def row_part(ks, sc, rm):
        for r in range(BLK // 64):
            m = rm[block(r, 64), :]
            s = sa[block(r, 64), :]
            for k in ks:
                s = s + (jnp.exp2(sc[k, block(r, 64), :128] - m) + jnp.exp2(sc[k, block(r, 64), 128:] - m))
            sa[block(r, 64), :] = s

    def one(b, xt, sc, rm, prev):
        left(b, xt)
        rm[...] = jnp.full_like(rm, -jnp.inf)
        for u in range(UNR):
            product(b, u, xt, sc, rm, cm)
        if prev is not None:
            sa[...] = jnp.zeros_like(sa)

        def some(g):
            for u in range(UNR):
                col_part(b, UNR * g + u, sc, cm)
            if prev is not None:
                row_part([UNR * g + u for u in range(UNR)], *prev)
            for u in range(UNR):
                product(b, lax.rem(UNR * g + UNR + u, SUPP), xt, sc, rm, cm)

        each(SUPP // UNR, some)
        rm[...] = jnp.broadcast_to(jnp.max(rm[...], 1, keepdims=True), (BLK, 128))
        if prev is not None:
            finish(b - 1, prev[1])

    def finish(b, rm):
        out = rm[...] + jnp.log2(jnp.sum(sa[...], 1, keepdims=True)) - math.log2(SUPP * BLK)
        for h in range(2):
            mine = fs[pl.ds(2 * b + h, 1), :]
            ff_ref[pl.ds(2 * b + h, 1), :] = (0.5 * UNIT) * (mine - (out[block(h), :].T[:1, :] - mine))

    one(0, xt0, sc0, rm0, None)

    def two(p):
        one(2 * p + 1, xt1, sc1, rm1, (sc0, rm0))
        one(2 * p + 2, xt0, sc0, rm0, (sc1, rm1))

    each(3, two)
    one(7, xt1, sc1, rm1, (sc0, rm0))

    def fill(p):
        for q in range(2):
            back[p, 2 * q:2 * q + 2, :] = lse[req_ref[p, 0, 2 + q]]

    each(DEV, fill)

    def ret_copy(d):
        to = lax.rem(me + d + 1, DEV)
        return remote(back.at[to], ret.at[me], ssem.at[d], rsem.at[d], place(to))

    pl.semaphore_wait(barrier, DEV - 1)
    each(DEV - 1, lambda d: ret_copy(d).start())
    mine = pltpu.make_async_copy(back.at[me], ret.at[me], lsem)
    mine.start()
    sa[...] = jnp.zeros_like(sa)

    each(SUPP // 2, lambda g: row_part((2 * g, 2 * g + 1), sc1, rm1))
    finish(7, rm1)
    lane = lax.broadcasted_iota(i32, (DEV, 128), 1).astype(f32)
    sub = lax.broadcasted_iota(i32, (DEV, 128), 0).astype(f32)
    hot, hot_t = [], []
    for q in range(2):
        idv = jnp.broadcast_to(inc_ref[:, 0, q:q + 1].astype(f32), (DEV, 128))
        idr[q] = idv
        hot.append(jnp.where(idv == lane, 1.0, 0.0).astype(bf16))
        hot_t.append(jnp.where(idv.T == sub, 1.0, 0.0).astype(bf16))
    count = sum(jnp.sum(h.astype(f32), 1, keepdims=True) for h in hot_t)
    mt[...] = jnp.zeros_like(mt)
    mine.wait()
    each(DEV - 1, lambda d: ret_copy(d).wait())
    for q in range(2):
        for h in range(2):
            ex[q, h] = ret[:, 2 * q + h, :]

    def tops(t):
        tf = t.astype(f32)
        for h in range(2):
            m = jnp.maximum(jnp.where(idr[0] == tf, ex[0, h], -jnp.inf), jnp.where(idr[1] == tf, ex[1, h], -jnp.inf))
            mt[h, pl.ds(t, 1), :] = jnp.max(m, 0, keepdims=True)

    each(TB_DEV, tops)
    for h in range(2):
        tot = jnp.zeros((DEV, 128), f32)
        mparts = split3(mt[h])
        for q in range(2):
            mx = sum(jnp.dot(hot[q], mp, preferred_element_type=f32) for mp in mparts)
            e = jnp.where(idr[q] >= 0.0, jnp.exp2(ex[q, h] - mx), 0.0)
            tot = tot + sum(jnp.dot(hot_t[q], ep, preferred_element_type=f32) for ep in split3(e))
        ex[0, h] = mt[h] + jnp.log2(tot) - jnp.log2(jnp.broadcast_to(count, (DEV, 128)) * BLK)
    for t in range(TB_DEV):
        for h in range(2):
            fg_ref[2 * t + h:2 * t + h + 1, :] = (0.5 * UNIT) * (sg[2 * t + h:2 * t + h + 1, :] - ex[0, h, t:t + 1, :])


def fine(slots, req, ftab, gtab, src_pts, src_cluster, tiles, tgt_cluster, incoming):
    S = jax.ShapeDtypeStruct
    V = pltpu.VMEM
    dma = pltpu.SemaphoreType.DMA
    return pl.pallas_call(
        fine_kernel,
        out_shape=(S((8, 128), f32), S((1, 128), f32), S((16, 128), f32), S((64, 128), f32)),
        in_specs=[SMEM, SMEM] + [VMEM] * 4 + [pl.BlockSpec(memory_space=pl.ANY)] + [VMEM] * 2,
        out_specs=(VMEM,) * 4,
        scratch_shapes=[V((DEV * 9, 8, 128), f32), V((2 * DEV, 128), f32), V((16, 128), f32), V((64, 128), f32),
                        V((2 * DEV, 128), f32), V((BLK, 128), bf16), V((BLK, 128), bf16), V((SUPP, 8, BLK), f32),
                        V((SUPP, BLK, BLK), f32), V((SUPP, BLK, BLK), f32), V((BLK, 128), f32), V((BLK, 128), f32),
                        V((BLK, 128), f32), V((DEV, 2, 128), f32), V((DEV, 4, 128), f32), V((DEV, 4, 128), f32),
                        V((2, DEV, 128), f32), V((2, DEV, 128), f32), V((2, 2, DEV, 128), f32),
                        dma((DEV,)), dma((DEV,)), dma, dma],
        compiler_params=pltpu.CompilerParams(collective_id=2, has_side_effects=True,
                                             vmem_limit_bytes=63 * 1024 * 1024),
        name="fine",
    )(slots, req, ftab, gtab, src_pts, src_cluster.reshape(16, 128), tiles.reshape(DEV * 9, 8, 128), tgt_cluster.reshape(64, 128), incoming)


def on_device(src_cent, tgt_cent, src_mass, tgt_mass, src_pts, tgt_pts, src_cluster, tgt_cluster, support):
    req, slots = make_requests(support)
    ftab, gtab, tiles, incoming = coarse(src_cent, src_mass, tgt_cent, tgt_mass, req, tgt_pts, tgt_cluster)
    cf, cg, ff, fg = fine(slots, req, ftab, gtab, src_pts, src_cluster, tiles, tgt_cluster, incoming)
    return cf.reshape(-1), cg.reshape(-1), ff.reshape(-1), fg.reshape(-1)


def solution(mesh):
    both = ("row", "col")
    in_specs = (P(None, "row"), P(None, "col"), P("row"), P("col"), P(None, both), P(None, both), P(both), P(both),
                P(both, None))
    out_specs = (P("row"), P("col"), P(both), P(both))
    return jax.shard_map(on_device, mesh=mesh, in_specs=in_specs, out_specs=out_specs, check_vma=False)
```

time: 193 us -> 164 us (0.85)
  Pallas kernels: 180 us -> 157 us
  local copies, waits for them, and re-layouts: 12.1 us -> 6.38 us
    pallas_call x1, Pallas kernels: 125 us -> 107 us  [coarse(): pl.pallas_call(coarse_kernel, out_shape=(S((32, 128), f32), S((32, 128),...]
    pallas_call x1, Pallas kernels: 54.1 us -> 47.9 us  [fine(): pl.pallas_call(fine_kernel, out_shape=(S((8, 128), f32), S((1, 128), f32)...]
    unnamed x22 -> x4, local copies, waits for them, and re-layouts: 10.8 us -> 5.11 us
where the time goes in v3:
time: 164 us
  Pallas kernels  157 us (96%)
  local copies, waits for them, and re-layouts  6.38 us (4%)
    pallas_call x1, Pallas kernels, coarse(): pl.pallas_call(coarse_kernel, out_shape=(S((32, 128), f32), S((32, 128),...  107 us
    pallas_call x1, Pallas kernels, fine(): pl.pallas_call(fine_kernel, out_shape=(S((8, 128), f32), S((1, 128), f32)...  47.9 us
    unnamed x4, local copies, waits for them, and re-layouts  5.11 us

profile of v3, /device:TPU:1, one launch (start us, length us, event | category | flops | bytes accessed | tf_op | source)
XLA Modules:
  0.0 163.7 jit_solution(12938587370276849942)
XLA Ops:
  0.6 1.3 reshape.41.sup_ref
  1.9 1.5 make_requests.1
  3.4 107.3 %coarse.1 = (f32[32,128]{1,0:T(8,128)}, f32[32,128]{1,0:T(8,128)}, f32[128,72,128]{2,1,0:T(8,128)}, s32[128,1,128]{2,1,0:T(1,128)}) custom-call(f32[16,1024]{1,0:T(8,128)} %src_in.1, f32[1,1024]{1,0:T(1,128)} %bitcast.16, f32[16,128]{1,0:T(8,128)} %tgt_in.1, f32[1,128]{1,0:T(1,128)} %bitcast.18, s32[128,1,128]{2,1,0:T(1,128)} %get-tuple-element.15.req_ref, ...), custom_call_target="tpu_custom_call" | custom-call | tf_op jit(solution)/shard_map/coarse/pallas_call | solution.py:324
  110.7 47.9 %fine.1 = (f32[8,128]{1,0:T(8,128)}, f32[1,128]{1,0:T(1,128)}, f32[16,128]{1,0:T(8,128)}, f32[64,128]{1,0:T(8,128)}) custom-call(s32[4,128]{1,0:T(4,128)} %get-tuple-element.14.slot_ref, s32[128,1,128]{2,1,0:T(1,128)} %get-tuple-element.15.req_ref, f32[32,128]{1,0:T(8,128)} %get-tuple-element.16.ftab_ref, f32[32,128]{1,0:T(8,128)} %get-tuple-element.17.gtab_ref, ...), custom_call_target="tpu_custom_call" | custom-call | tf_op jit(solution)/shard_map/fine/pallas_call | solution.py:553
  158.6 1.3 copy.17
  159.9 1.2 copy.18
  161.1 1.3 copy.19
  162.4 1.4 copy.20

commit v4 on v3

--- a/solution.py
+++ b/solution.py
@@ -82,11 +82,55 @@
     lax.fori_loop(0, n, step, 0)
 
 
-def coarse_kernel(src_in, smass_in, tgt_in, tmass_in, req_ref, pts_ref, clu_ref,
-                  ftab_ref, gtab_ref, tiles_ref, inc_ref,
-                  src_all, smass_all, tgt_all, tmass_all, inc_s, blocks, out_buf,
+def lookup(tab, idx):
+    low = idx & 127
+    high = idx >> 7
+    out = jnp.zeros((8, 128), f32)
+    for r in range(32):
+        got = jnp.take_along_axis(jnp.broadcast_to(tab[r:r + 1, :], (8, 128)), low, axis=1)
+        out = jnp.where(high == r, got, out)
+    return out
+
+
+def request_kernel(sup_ref, req_ref, slot_ref):
+    wanted = sup_ref[...].astype(f32)
+    owner = jnp.floor(wanted * (1.0 / TB_DEV))
+    local = wanted - owner * TB_DEV
+    sub = lax.broadcasted_iota(i32, (128, 128), 0)
+    lane = lax.broadcasted_iota(i32, (128, 128), 1)
+    lanef = lane.astype(f32)
+    same = jnp.broadcast_to(owner, (128, 128)) == sub.astype(f32)
+    lo = jnp.min(jnp.where(same, lanef, 1e6), 1, keepdims=True)
+    hi = jnp.max(jnp.where(same, lanef, -1.0), 1, keepdims=True)
+    locb = jnp.broadcast_to(local, (128, 128)) + 1.0
+    id0 = jnp.sum(jnp.where(lanef == lo, locb, 0.0), 1, keepdims=True) - 1.0
+    id1 = jnp.sum(jnp.where((lanef == hi) & (hi > lo), locb, 0.0), 1, keepdims=True) - 1.0
+    some = jnp.maximum(hi, 0.0)
+    row = jnp.where(lane == 0, id0, jnp.where(lane == 1, id1, jnp.where(lane == 2, jnp.minimum(lo, some), jnp.where(
+        lane == 3, some, jnp.where(lane == 4, jnp.maximum(id0, 0.0), jnp.maximum(id1, 0.0))))))
+    req_ref[:, 0, :] = row.astype(i32)
+    ownc = spread(owner)
+    before = jnp.where((ownc == jnp.broadcast_to(owner, (128, 128))) & (sub < lane), 1.0, 0.0)
+    second = jnp.sum(before, 0, keepdims=True)
+    out = jnp.concatenate([owner, second, owner, owner], 0)
+    slot_ref[...] = out.astype(i32)
+
+
+def make_requests(support):
+    return pl.pallas_call(
+        request_kernel,
+        out_shape=(jax.ShapeDtypeStruct((128, 1, 128), i32), jax.ShapeDtypeStruct((4, 128), i32)),
+        in_specs=[VMEM], out_specs=(VMEM, VMEM), name="make_requests",
+    )(support.reshape(1, 128))
+
+
+def kernel(req_s, slot_ref, req_ref, src_in, smass_in, tgt_in, tmass_in, pts_ref, clu_ref, src_ref, sclu_ref, oclu_ref,
+           out_ref,
+           ftab_ref, gtab_ref, tiles_ref, inc_ref,
+           src_all, smass_all, tgt_all, tmass_all, inc_s, blocks, out_buf,
                   a_scr, t0, t1, ys, xs, gp, lb, acc, fst, am, sh, mxs, rs, rbuf, fbuf,
-                  send_sem, recv_sem, cs_sem, cr_sem, qs_sem, qr_sem, bs_sem, br_sem, lsem):
+                  send_sem, recv_sem, cs_sem, cr_sem, qs_sem, qr_sem, bs_sem, br_sem, lsem,
+           gs, fs, sg, ccl, xt0, xt1, cm, sc0, sc1, rm0, rm1, sa, lse, back, ret, idr, mt, ex, ssem, rsem):
     row = lax.axis_index("row")
     col = lax.axis_index("col")
     me = row * 32 + col
@@ -119,6 +163,9 @@
         to = lax.rem(me + lax.rem((d + 1) * STRIDE, DEV), DEV)
         return remote(out_buf.at[to], tiles_ref.at[me], bs_sem.at[d], br_sem.at[d], place(to))
 
+    for t in range(TB_DEV):
+        for h in range(2):
+            blocks[t, h * 16:h * 16 + 16, :] = pts_ref[:, block(2 * t + h)]
     local = [pltpu.make_async_copy(tgt_in, tgt_all.at[col], lsem.at[0]),
              pltpu.make_async_copy(tmass_in, tmass_all.at[col], lsem.at[1]),
              pltpu.make_async_copy(src_in.at[:, quarter_of(row)], src_all.at[row], lsem.at[2]),
@@ -144,9 +191,9 @@
         tgt_copy(d, 0).wait()
         tgt_copy(d, 1).wait()
 
+    each(DEV - 1, lambda d: req_copy(d).start())
     each(3, start_src)
     each(31, start_tgt)
-    each(DEV - 1, lambda d: req_copy(d).start())
     for c in local:
         c.wait()
     each(3, wait_src)
@@ -162,9 +209,6 @@
             xs[r0:r0 + 128, :] = left_rows(src_all[q, :, block(h)])
             am[r0:r0 + 128, :] = spread(smass_all[q, :, block(h)])
 
-    for t in range(TB_DEV):
-        for h in range(2):
-            blocks[t, h * 16:h * 16 + 16, :] = pts_ref[:, block(2 * t + h)]
     each(DEV - 1, lambda d: req_copy(d).wait())
     to_scalar = pltpu.make_async_copy(inc_ref, inc_s, lsem.at[5])
     to_scalar.start()
@@ -179,8 +223,8 @@
 
     each(DEV, fill)
     each(43, lambda d: blk_copy(d).start())
-    own = pltpu.make_async_copy(out_buf.at[me], tiles_ref.at[me], lsem.at[6])
-    own.start()
+    own_block = pltpu.make_async_copy(out_buf.at[me], tiles_ref.at[me], lsem.at[6])
+    own_block.start()
 
     acc[...] = jnp.full_like(acc, -jnp.inf)
 
@@ -313,97 +357,15 @@
     for q in range(4):
         for i in range(4):
             ftab_ref[q * 8 + 2 * i:q * 8 + 2 * i + 2, :] = fbuf[i, 2 * q:2 * q + 2, :]
-    own.wait()
-    each(DEV - 1, lambda d: blk_copy(d).wait())
-
-
-def coarse(src_cent, src_mass, tgt_cent, tgt_mass, req, tgt_pts, tgt_cluster):
-    V = pltpu.VMEM
-    S = jax.ShapeDtypeStruct
-    dma = pltpu.SemaphoreType.DMA
-    return pl.pallas_call(
-        coarse_kernel,
-        out_shape=(S((32, 128), f32), S((32, 128), f32), S((DEV, 72, 128), f32), S((DEV, 1, 128), i32)),
-        in_specs=[VMEM] * 7,
-        out_specs=(VMEM, VMEM, pl.BlockSpec(memory_space=pl.ANY), VMEM),
-        scratch_shapes=[V((4, F, 256), f32), V((4, 1, 256), f32), V((32, F, 128), f32), V((32, 1, 128), f32),
-                        pltpu.SMEM((DEV, 1, 128), i32), V((TB_DEV, 32, 128), f32), V((DEV, 72, 128), f32),
-                        V((PART, KT), f32), V((CH, KT), f32), V((CH, KT), f32),
-                        V((128, KT), bf16), V((PART, 128), bf16), V((8, KT), f32), V((8, KT), f32), V((8, KT), f32),
-                        V((PART, 128), f32), V((PART, 128), f32), V((PART, 128), f32), V((256, 128), f32), V((CH, 128), f32),
-                        V((8, 4, 1, KT), f32), V((4, 8, 128), f32),
-                        dma((9, 3)), dma((9, 3)),
-                        dma((34, 2)), dma((34, 2)), dma((DEV,)), dma((DEV,)), dma((DEV,)), dma((DEV,)), dma((7,))],
-        compiler_params=pltpu.CompilerParams(collective_id=1, has_side_effects=True,
-                                             vmem_limit_bytes=62 * 1024 * 1024),
-        name="coarse",
-    )(src_cent, src_mass.reshape(1, -1), tgt_cent, tgt_mass.reshape(1, -1), req, tgt_pts,
-      tgt_cluster.reshape(TB_DEV, 2, 128))
-
-
-def request_kernel(sup_ref, req_ref, slot_ref):
-    wanted = sup_ref[...].astype(f32)
-    owner = jnp.floor(wanted * (1.0 / TB_DEV))
-    local = wanted - owner * TB_DEV
-    sub = lax.broadcasted_iota(i32, (128, 128), 0)
-    lane = lax.broadcasted_iota(i32, (128, 128), 1)
-    lanef = lane.astype(f32)
-    same = jnp.broadcast_to(owner, (128, 128)) == sub.astype(f32)
-    lo = jnp.min(jnp.where(same, lanef, 1e6), 1, keepdims=True)
-    hi = jnp.max(jnp.where(same, lanef, -1.0), 1, keepdims=True)
-    locb = jnp.broadcast_to(local, (128, 128)) + 1.0
-    id0 = jnp.sum(jnp.where(lanef == lo, locb, 0.0), 1, keepdims=True) - 1.0
-    id1 = jnp.sum(jnp.where((lanef == hi) & (hi > lo), locb, 0.0), 1, keepdims=True) - 1.0
-    some = jnp.maximum(hi, 0.0)
-    row = jnp.where(lane == 0, id0, jnp.where(lane == 1, id1, jnp.where(lane == 2, jnp.minimum(lo, some), jnp.where(
-        lane == 3, some, jnp.where(lane == 4, jnp.maximum(id0, 0.0), jnp.maximum(id1, 0.0))))))
-    req_ref[:, 0, :] = row.astype(i32)
-    ownc = spread(owner)
-    before = jnp.where((ownc == jnp.broadcast_to(owner, (128, 128))) & (sub < lane), 1.0, 0.0)
-    second = jnp.sum(before, 0, keepdims=True)
-    out = jnp.concatenate([owner * 9.0 + second * 4.0, second, owner * 9.0 + 8.0, owner], 0)
-    slot_ref[...] = out.astype(i32)
-
-
-def make_requests(support):
-    return pl.pallas_call(
-        request_kernel,
-        out_shape=(jax.ShapeDtypeStruct((128, 1, 128), i32), jax.ShapeDtypeStruct((4, 128), i32)),
-        in_specs=[VMEM], out_specs=(VMEM, VMEM), name="make_requests",
-    )(support.reshape(1, 128))
-
-
-def lookup(tab, idx):
-    low = idx & 127
-    high = idx >> 7
-    out = jnp.zeros((8, 128), f32)
-    for r in range(32):
-        got = jnp.take_along_axis(jnp.broadcast_to(tab[r:r + 1, :], (8, 128)), low, axis=1)
-        out = jnp.where(high == r, got, out)
-    return out
-
-
-def fine_kernel(slot_ref, req_ref, ftab_ref, gtab_ref, src_ref, sclu_ref, tile_hbm, oclu_ref, inc_ref,
-                cf_ref, cg_ref, ff_ref, fg_ref,
-                tile_ref, gs, fs, sg, ccl, xt0, xt1, cm, sc0, sc1, rm0, rm1, sa, lse, back, ret, idr, mt, ex,
-                ssem, rsem, lsem, tsem):
-    fetch = pltpu.make_async_copy(tile_hbm, tile_ref, tsem)
-    fetch.start()
-    row = lax.axis_index("row")
-    col = lax.axis_index("col")
-    me = row * 32 + col
-    barrier = pltpu.get_barrier_semaphore()
-    each(DEV - 1, lambda d: pl.semaphore_signal(barrier, inc=1, device_id=place(lax.rem(me + d + 1, DEV)),
-                                                device_id_type=MESH))
-    cf_ref[...] = ftab_ref[pl.ds(pl.multiple_of(row * 8, 8), 8), :]
-    cg_ref[...] = gtab_ref[pl.ds(col, 1), :]
+    out_ref[0:8, :] = ftab_ref[pl.ds(pl.multiple_of(row * 8, 8), 8), :]
+    out_ref[8:9, :] = gtab_ref[pl.ds(col, 1), :]
     ft = ftab_ref[...] * KAPPA
     gt = gtab_ref[...] * KAPPA
 
     def clusters(e):
-        both = tile_ref[slot_ref[2, e]]
+        pair = tiles_ref[slot_ref[2, e]]
         second = slot_ref[1, e].astype(f32) > 0.5
-        ccl[pl.ds(2 * e, 2), :] = jnp.where(second, both[2:4], both[0:2])
+        ccl[pl.ds(2 * e, 2), :] = jnp.where(second, pair[66:68], pair[64:66])
 
     for r in range(2):
         fs[block(r, 8), :] = lookup(ft, sclu_ref[block(r, 8), :])
@@ -413,7 +375,8 @@
         sg[rows, :] = lookup(gt, oclu_ref[rows, :])
 
     each(8, own)
-    fetch.wait()
+    own_block.wait()
+    each(DEV - 1, lambda d: blk_copy(d).wait())
     each(DEV, clusters)
 
     def sent(r):
@@ -430,11 +393,12 @@
     def duals(e):
         return [gs[pl.ds(2 * e + h, 1), :] for h in range(2)]
 
-    def product(b, k, xt, sc, rm, cm):
+    def pair_product(b, k, xt, sc, rm, cm):
         e = b * SUPP + k
-        i = slot_ref[0, e]
-        part = [jnp.concatenate([tile_ref[i + 2 * h], tile_ref[i + 2 * h + 1]], 0) for h in range(2)]
-        y = jnp.concatenate(part, 1)
+        i = slot_ref[2, e]
+        second = slot_ref[1, e].astype(f32) > 0.5
+        y = jnp.where(second, tiles_ref[i, 32:64, :], tiles_ref[i, 0:32, :])
+        y = jnp.concatenate([y[:16], y[16:]], 1)
         st = stack(y, jnp.concatenate(duals(e), 1) - KAPPA * jnp.sum(y * y, 0, keepdims=True), False)
         d = jnp.dot(xt[...], st, preferred_element_type=f32)
         sc[k] = d
@@ -460,7 +424,7 @@
         left(b, xt)
         rm[...] = jnp.full_like(rm, -jnp.inf)
         for u in range(UNR):
-            product(b, u, xt, sc, rm, cm)
+            pair_product(b, u, xt, sc, rm, cm)
         if prev is not None:
             sa[...] = jnp.zeros_like(sa)
 
@@ -470,7 +434,7 @@
             if prev is not None:
                 row_part([UNR * g + u for u in range(UNR)], *prev)
             for u in range(UNR):
-                product(b, lax.rem(UNR * g + UNR + u, SUPP), xt, sc, rm, cm)
+                pair_product(b, lax.rem(UNR * g + UNR + u, SUPP), xt, sc, rm, cm)
 
         each(SUPP // UNR, some)
         rm[...] = jnp.broadcast_to(jnp.max(rm[...], 1, keepdims=True), (BLK, 128))
@@ -481,7 +445,7 @@
         out = rm[...] + jnp.log2(jnp.sum(sa[...], 1, keepdims=True)) - math.log2(SUPP * BLK)
         for h in range(2):
             mine = fs[pl.ds(2 * b + h, 1), :]
-            ff_ref[pl.ds(2 * b + h, 1), :] = (0.5 * UNIT) * (mine - (out[block(h), :].T[:1, :] - mine))
+            out_ref[pl.ds(16 + 2 * b + h, 1), :] = (0.5 * UNIT) * (mine - (out[block(h), :].T[:1, :] - mine))
 
     one(0, xt0, sc0, rm0, None)
 
@@ -492,19 +456,18 @@
     each(3, two)
     one(7, xt1, sc1, rm1, (sc0, rm0))
 
-    def fill(p):
+    def fill_back(p):
         for q in range(2):
-            back[p, 2 * q:2 * q + 2, :] = lse[req_ref[p, 0, 2 + q]]
-
-    each(DEV, fill)
+            back[p, 2 * q:2 * q + 2, :] = lse[req_s[p, 0, 2 + q]]
+
+    each(DEV, fill_back)
 
     def ret_copy(d):
         to = lax.rem(me + d + 1, DEV)
         return remote(back.at[to], ret.at[me], ssem.at[d], rsem.at[d], place(to))
 
-    pl.semaphore_wait(barrier, DEV - 1)
     each(DEV - 1, lambda d: ret_copy(d).start())
-    mine = pltpu.make_async_copy(back.at[me], ret.at[me], lsem)
+    mine = pltpu.make_async_copy(back.at[me], ret.at[me], lsem.at[8])
     mine.start()
     sa[...] = jnp.zeros_like(sa)
 
@@ -543,34 +506,52 @@
         ex[0, h] = mt[h] + jnp.log2(tot) - jnp.log2(jnp.broadcast_to(count, (DEV, 128)) * BLK)
     for t in range(TB_DEV):
         for h in range(2):
-            fg_ref[2 * t + h:2 * t + h + 1, :] = (0.5 * UNIT) * (sg[2 * t + h:2 * t + h + 1, :] - ex[0, h, t:t + 1, :])
-
-
-def fine(slots, req, ftab, gtab, src_pts, src_cluster, tiles, tgt_cluster, incoming):
+            out_ref[32 + 2 * t + h:33 + 2 * t + h, :] = (0.5 * UNIT) * (sg[2 * t + h:2 * t + h + 1, :] - ex[0, h, t:t + 1, :])
+
+
+def split_kernel(all_ref, cf_ref, cg_ref, ff_ref, fg_ref):
+    cf_ref[...] = all_ref[0:8, :]
+    cg_ref[...] = all_ref[8:9, :]
+    ff_ref[...] = all_ref[16:32, :]
+    fg_ref[...] = all_ref[32:96, :]
+
+
+def on_device(src_cent, tgt_cent, src_mass, tgt_mass, src_pts, tgt_pts, src_cluster, tgt_cluster, support):
+    V = pltpu.VMEM
     S = jax.ShapeDtypeStruct
-    V = pltpu.VMEM
     dma = pltpu.SemaphoreType.DMA
-    return pl.pallas_call(
-        fine_kernel,
-        out_shape=(S((8, 128), f32), S((1, 128), f32), S((16, 128), f32), S((64, 128), f32)),
-        in_specs=[SMEM, SMEM] + [VMEM] * 4 + [pl.BlockSpec(memory_space=pl.ANY)] + [VMEM] * 2,
-        out_specs=(VMEM,) * 4,
-        scratch_shapes=[V((DEV * 9, 8, 128), f32), V((2 * DEV, 128), f32), V((16, 128), f32), V((64, 128), f32),
-                        V((2 * DEV, 128), f32), V((BLK, 128), bf16), V((BLK, 128), bf16), V((SUPP, 8, BLK), f32),
+    req, slots = make_requests(support)
+    out = pl.pallas_call(
+        kernel,
+        out_shape=S((96, 128), f32),
+        in_specs=[SMEM] * 2 + [VMEM] * 10,
+        out_specs=VMEM,
+        scratch_shapes=[V((32, 128), f32), V((32, 128), f32), V((DEV, 72, 128), f32),
+                        V((DEV, 1, 128), i32),
+                        V((4, F, 256), f32), V((4, 1, 256), f32), V((32, F, 128), f32), V((32, 1, 128), f32),
+                        pltpu.SMEM((DEV, 1, 128), i32), V((TB_DEV, 32, 128), f32), V((DEV, 72, 128), f32),
+                        V((PART, KT), f32), V((CH, KT), f32), V((CH, KT), f32),
+                        V((128, KT), bf16), V((PART, 128), bf16), V((8, KT), f32), V((8, KT), f32), V((8, KT), f32),
+                        V((PART, 128), f32), V((PART, 128), f32), V((PART, 128), f32), V((256, 128), f32),
+                        V((CH, 128), f32), V((8, 4, 1, KT), f32), V((4, 8, 128), f32),
+                        dma((9, 3)), dma((9, 3)), dma((34, 2)), dma((34, 2)),
+                        dma((DEV,)), dma((DEV,)), dma((DEV,)), dma((DEV,)), dma((9,)),
+                        V((2 * DEV, 128), f32), V((16, 128), f32), V((64, 128), f32), V((2 * DEV, 128), f32),
+                        V((BLK, 128), bf16), V((BLK, 128), bf16), V((SUPP, 8, BLK), f32),
                         V((SUPP, BLK, BLK), f32), V((SUPP, BLK, BLK), f32), V((BLK, 128), f32), V((BLK, 128), f32),
                         V((BLK, 128), f32), V((DEV, 2, 128), f32), V((DEV, 4, 128), f32), V((DEV, 4, 128), f32),
                         V((2, DEV, 128), f32), V((2, DEV, 128), f32), V((2, 2, DEV, 128), f32),
-                        dma((DEV,)), dma((DEV,)), dma, dma],
-        compiler_params=pltpu.CompilerParams(collective_id=2, has_side_effects=True,
+                        dma((DEV,)), dma((DEV,))],
+        compiler_params=pltpu.CompilerParams(collective_id=1, has_side_effects=True,
                                              vmem_limit_bytes=63 * 1024 * 1024),
-        name="fine",
-    )(slots, req, ftab, gtab, src_pts, src_cluster.reshape(16, 128), tiles.reshape(DEV * 9, 8, 128), tgt_cluster.reshape(64, 128), incoming)
-
-
-def on_device(src_cent, tgt_cent, src_mass, tgt_mass, src_pts, tgt_pts, src_cluster, tgt_cluster, support):
-    req, slots = make_requests(support)
-    ftab, gtab, tiles, incoming = coarse(src_cent, src_mass, tgt_cent, tgt_mass, req, tgt_pts, tgt_cluster)
-    cf, cg, ff, fg = fine(slots, req, ftab, gtab, src_pts, src_cluster, tiles, tgt_cluster, incoming)
+        name="transport",
+    )(req, slots, req, src_cent, src_mass.reshape(1, -1), tgt_cent, tgt_mass.reshape(1, -1), tgt_pts,
+      tgt_cluster.reshape(TB_DEV, 2, 128), src_pts, src_cluster.reshape(16, 128), tgt_cluster.reshape(64, 128))
+    cf, cg, ff, fg = pl.pallas_call(
+        split_kernel,
+        out_shape=(S((8, 128), f32), S((1, 128), f32), S((16, 128), f32), S((64, 128), f32)),
+        in_specs=[VMEM], out_specs=(VMEM,) * 4, name="split",
+    )(out)
     return cf.reshape(-1), cg.reshape(-1), ff.reshape(-1), fg.reshape(-1)
 
 

time: 164 us -> 157 us (0.957)
  local copies, waits for them, and re-layouts: 6.38 us -> 1.27 us
  Pallas kernels: 157 us -> 155 us
    unnamed x4 -> x2, local copies, waits for them, and re-layouts: 5.11 us -> 0.68 us
where the time goes in v4:
time: 157 us
  Pallas kernels  155 us (99%)
    pallas_call x1, Pallas kernels, on_device(): pl.pallas_call(kernel, out_shape=S((96, 128), f32), in_specs=[SMEM] * 2 +...  152 us

profile of v4, /device:TPU:1, one launch (start us, length us, event | category | flops | bytes accessed | tf_op | source)
XLA Modules:
  0.0 157.2 jit_solution(12043648912487523276)
XLA Ops:
  0.6 0.0 copy-start
  0.6 0.7 copy-done
  1.3 0.6 reshape.38.sup_ref
  1.9 1.5 make_requests.1
  3.4 152.3 %transport.1.all_ref = f32[96,128]{1,0:T(8,128)} custom-call(s32[128,1,128]{2,1,0:T(1,128)} %get-tuple-element.10.req_s.req_ref, s32[4,128]{1,0:T(4,128)} %get-tuple-element.11.slot_ref, s32[128,1,128]{2,1,0:T(1,128)} %get-tuple-element.10.req_s.req_ref, f32[16,1024]{1,0:T(8,128)} %src_in.1, f32[1,1024]{1,0:T(1,128)} %bitcast.12, f32[16,128]{1,0:T(8,128)} %tgt_in.1, ...), custom_call_target="tpu_custom_call" | custom-call | tf_op jit(solution)/shard_map/transport/pallas_call | solution.py:524
  155.7 1.4 split.1
Async XLA Ops:
  0.6 0.7 copy-start

commit v5 on v4

--- a/solution.py
+++ b/solution.py
@@ -222,7 +222,7 @@
         out_buf[p, 68:72, :] = jnp.zeros((4, 128), f32)
 
     each(DEV, fill)
-    each(43, lambda d: blk_copy(d).start())
+    each(71, lambda d: blk_copy(d).start())
     own_block = pltpu.make_async_copy(out_buf.at[me], tiles_ref.at[me], lsem.at[6])
     own_block.start()
 
@@ -285,7 +285,7 @@
         for c in copies:
             c.start()
         if send:
-            each(12, lambda d: blk_copy(43 + 12 * k + d).start())
+            each(8, lambda d: blk_copy(71 + 8 * k + d).start())
         for c in copies:
             c.wait()
 

time: 157 us -> 165 us (1.051)
  Pallas kernels: 155 us -> 163 us
    pallas_call x1, Pallas kernels: 152 us -> 160 us  [on_device(): pl.pallas_call(kernel, out_shape=S((96, 128), f32), in_specs=[SMEM] * 2 +...]
where the time goes in v5:
time: 165 us
  Pallas kernels  163 us (99%)
    pallas_call x1, Pallas kernels, on_device(): pl.pallas_call(kernel, out_shape=S((96, 128), f32), in_specs=[SMEM] * 2 +...  160 us

profile of v5, /device:TPU:1, one launch (start us, length us, event | category | flops | bytes accessed | tf_op | source)
XLA Modules:
  0.0 164.6 jit_solution(2307950353032847285)
XLA Ops:
  0.6 0.0 copy-start
  0.6 0.7 copy-done
  1.3 0.6 reshape.38.sup_ref
  1.9 1.5 make_requests.1
  3.4 159.8 %transport.1.all_ref = f32[96,128]{1,0:T(8,128)} custom-call(s32[128,1,128]{2,1,0:T(1,128)} %get-tuple-element.10.req_s.req_ref, s32[4,128]{1,0:T(4,128)} %get-tuple-element.11.slot_ref, s32[128,1,128]{2,1,0:T(1,128)} %get-tuple-element.10.req_s.req_ref, f32[16,1024]{1,0:T(8,128)} %src_in.1, f32[1,1024]{1,0:T(1,128)} %bitcast.12, f32[16,128]{1,0:T(8,128)} %tgt_in.1, ...), custom_call_target="tpu_custom_call" | custom-call | tf_op jit(solution)/shard_map/transport/pallas_call | solution.py:524
  163.2 1.4 split.1
Async XLA Ops:
  0.6 0.7 copy-start
